TPU v7x, 32 devices: a whole 2x2x4 slice. The times are simulated.
32 devices in a mesh: groups: 2 (over y), enrol: 4 (over z), probe: 4 (over x, core).
Axes of the slice: x: 2, y: 2, z: 4, core: 2. Of those that a mesh axis runs over, the one named last changes fastest.
Arguments:
- images: float32 [16384, 512], P(('groups', 'enrol', 'probe')), parts along dimension 0, may hold values from -6 to 6
- w_first: float32 [512, 2048], replicated, may hold values from -0.25 to 0.25
- w_second: float32 [2048, 256], replicated, may hold values from -0.125 to 0.125
- calib_scale: float32 [1], replicated, may hold values from 5 to 20
- calib_bias: float32 [1], replicated, may hold values from -2 to 2
- template_slot: int32 [16384], P(('groups', 'enrol', 'probe')), parts along dimension 0, may hold values from 0 to 191
- media_counts: int32 [32, 16], P(('groups', 'enrol', 'probe')), parts along dimension 0, may hold values from 1 to 64, as said below
Outputs:
- scores: bfloat16 [4096, 1024], P(('groups', 'enrol'), 'probe'), parts along dimension 0
There are 2 independent parts, one for each index of `groups`. A program takes and returns all parts, laid end to end along the dimension named above; an argument that names none is the same for every part. Nothing has to cross between parts.
Inputs may be any that keep to these rules, and one draw needn't show every extreme that they name: `media_counts`: each row sums to 512; in every draw one owner receives exactly 64 images from every device.
All inputs are finite; a program needn't handle non-finite values.
Results may differ from a plain program's by a relative error of at most 0.001.
Values sent between devices are 32-bit elements; how exact they have to be, the bound alone decides.
No kernel may reach another device: no remote copies, remote signals or barrier semaphores. Data moves between devices by JAX's collectives and lax.ppermute only.
A program may use at most 64 MiB of HBM per device.

v0:
```python
import jax
import jax.numpy as jnp
from jax import lax
from jax.sharding import PartitionSpec as P

ET_OWN = 128
PT_OWN = 64


HIGH = lax.Precision.HIGHEST


def unit_rows(table):
    return table * lax.rsqrt(jnp.sum(table * table, axis=-1, keepdims=True) + 1e-06)


def shards(images, w_first, w_second, calib_scale, calib_bias, template_slot, media_counts):
    owners = media_counts.shape[1]
    local_images = images.shape[0]
    capacity = 2 * local_images // owners
    width = w_second.shape[1]
    hidden = jax.nn.gelu(
        jnp.dot(images, w_first, precision=HIGH, preferred_element_type=jnp.float32)
    )
    feature = jnp.dot(hidden, w_second, precision=HIGH, preferred_element_type=jnp.float32)
    embedding = unit_rows(feature)
    counts = media_counts[0]
    starts = jnp.cumsum(counts) - counts
    offsets = jnp.arange(capacity, dtype=jnp.int32)
    filled = offsets[None, :] < counts[:, None]
    picked = jnp.where(filled, starts[:, None] + offsets[None, :], 0).reshape(-1)
    send_rows = embedding[picked].reshape(owners, capacity, width) * filled[:, :, None].astype(
        jnp.float32
    )
    send_slots = jnp.where(filled, template_slot[picked].reshape(owners, capacity), -1)
    got_rows, got_slots = (
        lax.all_to_all(send_rows, ("enrol", "probe"), split_axis=0, concat_axis=0, tiled=True),
        lax.all_to_all(send_slots, ("enrol", "probe"), split_axis=0, concat_axis=0, tiled=True),
    )
    got_rows = got_rows.reshape(owners * capacity, width)
    got_slots = got_slots.reshape(owners * capacity)
    slot_count = ET_OWN + PT_OWN
    selector = (got_slots[None, :] == jnp.arange(slot_count, dtype=jnp.int32)[:, None]).astype(
        jnp.float32
    )
    pooled = jnp.dot(selector, got_rows, precision=HIGH, preferred_element_type=jnp.float32)
    templates = unit_rows(pooled)
    enrol_own = templates[:ET_OWN]
    probe_own = templates[ET_OWN:]
    enrol_block = lax.all_gather(enrol_own, "probe", axis=0, tiled=True)
    slope = calib_scale[0]
    offset = calib_bias[0]
    cosine = jnp.dot(
        enrol_block,
        lax.all_gather(probe_own, "enrol", axis=0, tiled=True).T,
        precision=HIGH,
        preferred_element_type=jnp.float32,
    )
    return jax.nn.sigmoid(slope * cosine + offset).astype(jnp.bfloat16)


def solution(mesh):
    return jax.shard_map(
        shards,
        mesh=mesh,
        in_specs=(
            P(("groups", "enrol", "probe"), None),
            P(),
            P(),
            P(),
            P(),
            P(("groups", "enrol", "probe")),
            P(("groups", "enrol", "probe"), None),
        ),
        out_specs=P(("groups", "enrol"), "probe"),
        check_vma=False,
    )
```

profile of v0, /device:TPU:0, one launch (start us, length us, event | category | flops | bytes accessed | tf_op | source)
XLA Modules:
  0.0 92.5 jit_solution(2711061738317746428)
XLA Ops:
  0.0 0.0 copy-start
  0.0 0.0 copy-start.2
  0.0 0.9 copy.10
  0.9 0.1 reduce
  1.0 0.7 bitcast_subtract_fusion
  1.7 0.7 add_select_fusion
  2.4 0.1 select_n.37
  2.5 6.2 %gather_fusion = s32[1024]{0:T(1024)S(1)} fusion(s32[512]{0:T(512)} %param.12, s32[1024]{0:T(1024)S(1)} %broadcast_clamp_fusion), kind=kCustom, calls=%fused_computation | custom fusion | bytes 12288 | tf_op jit(solution)/shard_map/gather | solution.py:35
  8.7 0.1 reshape.184
  8.8 0.0 copy-done.2
  8.8 0.7 compare_select_fusion
  9.5 7.4 %all-to-all-start = ((s32[16,1,64]{2,1,0:T(1,128)}), s32[16,1,64]{2,1,0:T(1,128)S(1)}, u32[]{:S(2)}, u32[]{:S(2)}) async-start(s32[16,1,64]{2,1,0:T(1,128)} %compare_select_fusion), calls=%async_computation | async-start | bytes 16384 | tf_op jit(solution)/shard_map/all_to_all | solution.py:38
  16.9 0.1 fusion.21
  17.0 0.0 copy-done.1
  17.0 8.8 %fusion.26 = f32[512,2048]{1,0:T(8,128)S(1)} fusion(f32[512,512]{1,0:T(8,128)S(1)} %copy-done.1, f32[512,2048]{1,0:T(8,128)} %param.8), kind=kOutput, calls=%fused_computation.43 | convolution fusion | flops 6442450944 | bytes 9437184 | tf_op jit(solution)/shard_map/dot_general | solution.py:23
  25.8 0.0 copy-done
  25.8 5.1 %multiply_reduce_fusion = (f32[512]{0:T(512)S(1)}, f32[512,256]{0,1:T(8,128)S(1)}) fusion(f32[2048,256]{1,0:T(8,128)S(1)} %copy-done, f32[512,2048]{1,0:T(8,128)S(1)} %fusion.26), kind=kOutput, calls=%fused_computation.25 | convolution fusion | flops 3229875712 | bytes 6817792 | tf_op jit(solution)/shard_map/dot_general | solution.py:25
  30.9 0.1 broadcast_multiply_fusion.1
  30.9 0.2 copy.11
  31.1 4.7 %gather_fusion.1 = f32[1024,256]{1,0:T(8,128)} fusion(f32[512,256]{1,0:T(8,128)S(1)} %copy.11, s32[1024]{0:T(1024)S(1)} %broadcast_clamp_fusion), kind=kCustom, calls=%fused_computation.1 | custom fusion | bytes 2101248 | tf_op jit(solution)/shard_map/gather | solution.py:32
  35.8 2.4 %broadcast_multiply_fusion = f32[16,64,256]{2,1,0:T(8,128)} fusion(f32[16,64,256]{2,1,0:T(8,128)} %bitcast.16, f32[16,64]{1,0:T(8,128)S(1)} %fusion.21), kind=kLoop, calls=%fused_computation.24 | loop fusion | flops 262144 | bytes 2101248 | tf_op jit(solution)/shard_map/mul | solution.py:32
  38.2 0.0 all-to-all-done
  38.2 6.0 %all-to-all-start.1 = ((f32[16,64,256]{2,1,0:T(8,128)}), f32[16,64,256]{2,1,0:T(8,128)S(1)}, u32[]{:S(2)}, u32[]{:S(2)}) async-start(f32[16,64,256]{2,1,0:T(8,128)} %broadcast_multiply_fusion), calls=%async_computation.1 | async-start | bytes 2097152 | tf_op jit(solution)/shard_map/all_to_all | solution.py:37
  45.5 0.5 broadcast.96
  46.1 0.7 reduce.4
  46.7 0.1 eq.15
  46.8 20.3 %all-to-all-done.1 = f32[16,64,256]{2,1,0:T(8,128)S(1)} async-done(((f32[16,64,256]{2,1,0:T(8,128)}), f32[16,64,256]{2,1,0:T(8,128)S(1)}, u32[]{:S(2)}, u32[]{:S(2)}) %all-to-all-start.1) | async-done | bytes 1048608 | tf_op jit(solution)/shard_map/all_to_all | solution.py:37
  67.1 0.8 multiply_reduce_fusion.1
  67.9 0.1 broadcast_multiply_fusion.2
  68.1 7.9 %all_gather.6 = f32[512,256]{1,0:T(8,128)S(1)} all-gather(f32[128,256]{1,0:T(8,128)S(1)} %slice.12), channel_id=1, replica_groups=mesh['groups'=2,'enrol'=4,'probe'=4] {'probe'}, dimensions={0}, use_global_device_ids=true | all-gather | bytes 655360 | tf_op jit(solution)/shard_map/all_gather | solution.py:50
  75.9 15.2 %all_gather.7 = f32[256,256]{1,0:T(8,128)S(1)} all-gather(f32[64,256]{1,0:T(8,128)S(1)} %slice.13), channel_id=1, replica_groups=mesh['groups'=2,'enrol'=4,'probe'=4] {'enrol'}, dimensions={0}, use_global_device_ids=true | all-gather | bytes 327680 | tf_op jit(solution)/shard_map/all_gather | solution.py:55
  91.1 1.4 %fusion.18 = bf16[512,256]{1,0:T(8,128)(2,1)} fusion(f32[512,256]{1,0:T(8,128)S(1)} %all_gather.6, f32[256,256]{1,0:T(8,128)S(1)} %all_gather.7, f32[]{:T(128)} %bitcast.15, f32[]{:T(128)} %bitcast.14), kind=kOutput, calls=%fused_computation.21 | convolution fusion | flops 403439616 | bytes 1048584 | tf_op jit(solution)/shard_map/dot_general | solution.py:53
  (8 shorter events, 0.1 us)
Async XLA Ops:
  0.0 25.8 %copy-start = (f32[2048,256]{1,0:T(8,128)S(1)}, f32[2048,256]{1,0:T(8,128)}, u32[]{:S(2)}) copy-start(f32[2048,256]{1,0:T(8,128)} %param.9) | copy-start | bytes 6291460
  0.0 8.8 %copy-start.2 = (s32[1,16]{1,0:T(1,128)S(1)}, s32[1,16]{1,0:T(1,128)}, u32[]{:S(2)}) copy-start(s32[1,16]{1,0:T(1,128)} %param.13) | copy-start | bytes 196
  0.0 16.9 %copy-start.1 = (f32[512,512]{1,0:T(8,128)S(1)}, f32[512,512]{1,0:T(8,128)}, u32[]{:S(2)}) copy-start(f32[512,512]{1,0:T(8,128)} %param.7) | copy-start | bytes 3145732
  9.5 28.8 %all-to-all-start = ((s32[16,1,64]{2,1,0:T(1,128)}), s32[16,1,64]{2,1,0:T(1,128)S(1)}, u32[]{:S(2)}, u32[]{:S(2)}) async-start(s32[16,1,64]{2,1,0:T(1,128)} %compare_select_fusion), calls=%async_computation | async-start | bytes 16384 | tf_op jit(solution)/shard_map/all_to_all | solution.py:38
  38.2 28.9 %all-to-all-start.1 = ((f32[16,64,256]{2,1,0:T(8,128)}), f32[16,64,256]{2,1,0:T(8,128)S(1)}, u32[]{:S(2)}, u32[]{:S(2)}) async-start(f32[16,64,256]{2,1,0:T(8,128)} %broadcast_multiply_fusion), calls=%async_computation.1 | async-start | bytes 2097152 | tf_op jit(solution)/shard_map/all_to_all | solution.py:37
where the time goes:
time: 92.9 us; the launch traced here: 92.5 us
  blocking collectives  23.1 us (25%)
  waiting for transfers between devices  20.3 us (22%)
  matrix products  16 us (17%)
  starting transfers between devices  13.4 us (14%)
  local copies, waits for them, and re-layouts  12.7 us (14%)
  other arithmetic  5.57 us (6%)
  between operations  1.41 us (2%)
    all_to_all x1, waiting for transfers between devices, shards(): lax.all_to_all(send_rows, ('enrol', 'probe'), split_axis=0, concat_axis=0...  20.3 us
    all_gather x1, blocking collectives, shards(): lax.all_gather(probe_own, 'enrol', axis=0, tiled=True)  15.2 us
    dot_general x1, matrix products, shards(): jnp.dot(images, w_first, precision=HIGH, preferred_element_type=jnp.float32)  8.8 us
    all_gather x1, blocking collectives, shards(): enrol_block = lax.all_gather(enrol_own, 'probe', axis=0, tiled=True)  7.88 us
    all_to_all x1, starting transfers between devices, shards(): lax.all_to_all(send_slots, ('enrol', 'probe'), split_axis=0, concat_axis=...  7.39 us
    gather x1, local copies, waits for them, and re-layouts, shards(): template_slot[picked].reshape(owners, capacity)  6.18 us
    all_to_all x1, starting transfers between devices, shards(): lax.all_to_all(send_rows, ('enrol', 'probe'), split_axis=0, concat_axis=0...  6.01 us
    dot_general x1, matrix products, shards(): jnp.dot(hidden, w_second, precision=HIGH, preferred_element_type=jnp.floa...  5.09 us
  transfers between devices with their start and end apart: 2, of which 1 were waited for; matrix products, arithmetic and copies ran while one was open for 24% of the time, Pallas kernels for 0%

commit v1 on v0

v1 whole, which is shorter than its diff:
```python
import functools

import jax
import jax.numpy as jnp
from jax import lax
from jax.experimental import pallas as pl
from jax.experimental.pallas import tpu as pltpu
from jax.sharding import PartitionSpec as P

ET_OWN = 128
PT_OWN = 64
SLOTS = ET_OWN + PT_OWN
NONE = -4096
EPS = 1e-06
LANES = 128
CHUNK = 256
F32 = jnp.float32
BF16 = jnp.bfloat16


def split(value):
    high = value.astype(BF16)
    return high, (value - high.astype(F32)).astype(BF16)


def unit(table):
    return table * lax.rsqrt(jnp.sum(table * table, axis=-1, keepdims=True) + EPS)


def dot(a, b, dims=((1,), (0,))):
    return lax.dot_general(a, b, (dims, ((), ())), preferred_element_type=F32)


def place(n_enrol, n_probe):
    z, p = lax.axis_index("enrol"), lax.axis_index("probe")
    rows, chips = n_enrol // 2, n_probe // 2
    return z // rows, (z % rows) * chips + p // 2, p % 2


def embed_kernel(n_enrol, n_probe, count, slots, images, w_first, w_second, *rest):
    chips = n_enrol * n_probe // 4
    owners = n_enrol * n_probe
    far, near = rest[:chips], rest[chips : 2 * chips]
    (img, w1, w2, emb, table, ends, sem_img, sem_w1, sem_w2) = rest[2 * chips :]
    n_img, d_in = images.shape
    width = w_second.shape[1]
    pieces = w1.shape[0]
    block = near[0].shape[0]
    copy_img = pltpu.make_async_copy(images, img, sem_img)
    copy_img.start()
    copies = []
    for j in range(pieces):
        a = pltpu.make_async_copy(w_first.at[:, pl.ds(j * CHUNK, CHUNK)], w1.at[j], sem_w1.at[j])
        b = pltpu.make_async_copy(w_second.at[pl.ds(j * CHUNK, CHUNK)], w2.at[j], sem_w2.at[j])
        a.start()
        b.start()
        copies.append((a, b))

    ends[0] = 0
    rows = slots.shape[0]
    position = lax.broadcasted_iota(jnp.int32, (rows, LANES), 0) * LANES
    position = position + lax.broadcasted_iota(jnp.int32, (rows, LANES), 1)
    odd = jnp.zeros((rows, LANES), jnp.int32)
    total = jnp.int32(0)
    for o in range(owners):
        total = total + count[0, o]
        ends[o + 1] = total
        odd = jnp.where(position >= total, (o + 1) % 2, odd)
    table[...] = jnp.full(table.shape, NONE, jnp.int32)
    table[0:rows, :] = slots[...] + SLOTS * odd

    copy_img.wait()
    x_high, x_low = split(img[...])
    feature = jnp.zeros((n_img, width), F32)
    for j in range(pieces):
        copies[j][0].wait()
        w_high, w_low = split(w1[j])
        pre = dot(x_high, w_high) + dot(x_low, w_high) + dot(x_high, w_low)
        h_high, h_low = split(jax.nn.gelu(pre))
        copies[j][1].wait()
        v_high, v_low = split(w2[j])
        feature = feature + (dot(h_high, v_high) + dot(h_low, v_high) + dot(h_high, v_low))
    feature = unit(feature)
    tiles = width // LANES
    for t in range(tiles):
        emb[t, 0:n_img, :] = feature[:, t * LANES : (t + 1) * LANES]
        emb[t, n_img : n_img + block, :] = jnp.zeros((block, LANES), F32)

    half, chip, _ = place(n_enrol, n_probe)
    lane = lax.broadcasted_iota(jnp.int32, (1, LANES), 1)

    def window(start, size):
        row, shift = start // LANES, start % LANES
        back = (LANES - shift) % LANES
        one = pltpu.roll(table[pl.ds(row, 1), :], back, 1)
        two = pltpu.roll(table[pl.ds(row + 1, 1), :], back, 1)
        ids = jnp.where(lane < LANES - shift, one, two)
        return jnp.where(lane < size, ids, NONE).astype(F32)

    for k in range(chips):
        to = chip ^ k
        for side in range(2):
            pair = (half if side else 1 - half) * chips + to
            start, stop = ends[2 * pair], ends[2 * pair + 2]
            out = near[k] if side else far[k]
            for t in range(tiles):
                out[0:block, t * LANES : (t + 1) * LANES] = emb[t, pl.ds(start, block), :]
            far[k][block + side : block + side + 1, 0:LANES] = window(start, stop - start)


def embed(n_enrol, n_probe, images, w_first, w_second, slots, count):
    chips = n_enrol * n_probe // 4
    n_img, d_in = images.shape
    width = w_second.shape[1]
    pieces = w_second.shape[0] // CHUNK
    block = 4 * n_img // (n_enrol * n_probe)
    vmem = pl.BlockSpec(memory_space=pltpu.VMEM)
    hbm = pl.BlockSpec(memory_space=pl.ANY)
    outs = pl.pallas_call(
        functools.partial(embed_kernel, n_enrol, n_probe),
        out_shape=[jax.ShapeDtypeStruct((block + 8, width), F32)] * chips
        + [jax.ShapeDtypeStruct((block, width), F32)] * chips,
        in_specs=[pl.BlockSpec(memory_space=pltpu.SMEM), vmem, hbm, hbm, hbm],
        out_specs=[vmem] * (2 * chips),
        scratch_shapes=[
            pltpu.VMEM((n_img, d_in), F32),
            pltpu.VMEM((pieces, d_in, CHUNK), F32),
            pltpu.VMEM((pieces, CHUNK, width), F32),
            pltpu.VMEM((width // LANES, n_img + block, LANES), F32),
            pltpu.VMEM((n_img // LANES + 8 - n_img // LANES % 8, LANES), jnp.int32),
            pltpu.SMEM((n_enrol * n_probe + 1,), jnp.int32),
            pltpu.SemaphoreType.DMA,
            pltpu.SemaphoreType.DMA((pieces,)),
            pltpu.SemaphoreType.DMA((pieces,)),
        ],
        compiler_params=pltpu.CompilerParams(vmem_limit_bytes=24 << 20),
        name="embed",
    )(count, slots.reshape(n_img // LANES, LANES), images, w_first, w_second)
    return outs[:chips], outs[chips:]


def pool_kernel(n_enrol, n_probe, side, *refs):
    chips = n_enrol * n_probe // 4
    rows, ids = refs[:chips], refs[chips : 2 * chips]
    mine, other = refs[2 * chips :]
    _, _, core = place(n_enrol, n_probe)
    block = rows[0].shape[0] - (0 if side else 8)
    first = block - 0
    slot = lax.broadcasted_iota(jnp.int32, (2 * SLOTS, block), 0)
    total = jnp.zeros((2 * SLOTS, mine.shape[1]), F32)
    for k in range(chips):
        at = first + side
        want = ids[k][at : at + 1, 0:LANES][:, :block].astype(jnp.int32)
        moved = want - core * SLOTS
        want = jnp.where((want >= 0) & (moved < 0), moved + 2 * SLOTS, moved)
        pick = (slot == want).astype(F32).astype(BF16)
        high, low = split(rows[k][0:block, :])
        total = total + dot(pick, high) + dot(pick, low)
    mine[...] = total[:SLOTS]
    other[...] = total[SLOTS:]


def pool(n_enrol, n_probe, side, rows, ids):
    width = rows[0].shape[1]
    vmem = pl.BlockSpec(memory_space=pltpu.VMEM)
    return pl.pallas_call(
        functools.partial(pool_kernel, n_enrol, n_probe, side),
        out_shape=[jax.ShapeDtypeStruct((SLOTS, width), F32)] * 2,
        in_specs=[vmem] * (2 * len(rows)),
        out_specs=[vmem] * 2,
        compiler_params=pltpu.CompilerParams(vmem_limit_bytes=8 << 20),
        name="pool_near" if side else "pool_far",
    )(*rows, *ids)


def score_kernel(n_enrol, n_probe, scale, bias, *refs):
    rows, cols = n_enrol // 2, n_probe // 2
    enrol, probe = refs[: 2 * cols], refs[2 * cols : 2 * cols + rows]
    out, table = refs[2 * cols + rows :]
    z, p = lax.axis_index("enrol"), lax.axis_index("probe")
    for k in range(rows):
        own = (z ^ k) * PT_OWN
        across = (z ^ k ^ rows) * PT_OWN
        table[pl.ds(pl.multiple_of(own, PT_OWN), PT_OWN), :] = unit(probe[k][0:PT_OWN, :])
        table[pl.ds(pl.multiple_of(across, PT_OWN), PT_OWN), :] = unit(probe[k][PT_OWN:, :])
    p_high, p_low = split(table[...])
    slope, offset = scale[0], bias[0]
    last = ((1,), (1,))
    for k in range(n_probe):
        e_high, e_low = split(unit(enrol[k][...]))
        cosine = dot(e_high, p_high, last) + dot(e_low, p_high, last) + dot(e_high, p_low, last)
        at = pl.multiple_of((p ^ k) * ET_OWN, ET_OWN)
        out[pl.ds(at, ET_OWN), :] = jax.nn.sigmoid(slope * cosine + offset).astype(BF16)


def score(n_enrol, n_probe, scale, bias, enrol, probe):
    width = enrol[0].shape[1]
    vmem = pl.BlockSpec(memory_space=pltpu.VMEM)
    smem = pl.BlockSpec(memory_space=pltpu.SMEM)
    return pl.pallas_call(
        functools.partial(score_kernel, n_enrol, n_probe),
        out_shape=jax.ShapeDtypeStruct((n_probe * ET_OWN, n_enrol * PT_OWN), BF16),
        in_specs=[smem, smem] + [vmem] * (len(enrol) + len(probe)),
        out_specs=vmem,
        scratch_shapes=[pltpu.VMEM((n_enrol * PT_OWN, width), F32)],
        compiler_params=pltpu.CompilerParams(vmem_limit_bytes=8 << 20),
        name="score",
    )(scale, bias, *enrol, *probe)


def solution(mesh):
    n_enrol, n_probe = mesh.shape["enrol"], mesh.shape["probe"]
    rows, cols = n_enrol // 2, n_probe // 2
    chips = rows * cols

    def flip(value, enrol_bits, probe_bits):
        pairs = [
            (z * n_probe + p, (z ^ enrol_bits) * n_probe + (p ^ probe_bits))
            for z in range(n_enrol)
            for p in range(n_probe)
        ]
        return lax.ppermute(value, ("enrol", "probe"), pairs)

    def across_chips(blocks):
        return [blocks[0]] + [
            flip(blocks[k], k // cols, 2 * (k % cols)) for k in range(1, chips)
        ]

    def shards(images, w_first, w_second, scale, bias, template_slot, media_counts):
        far, near = embed(n_enrol, n_probe, images, w_first, w_second, template_slot, media_counts)
        far = across_chips(far)
        near = across_chips(near)
        mine, other = pool(n_enrol, n_probe, 0, far, far)
        far_sum = mine + flip(other, 0, 1)
        from_far = flip(far_sum, rows, 0)
        mine, other = pool(n_enrol, n_probe, 1, near, far)
        near_sum = mine + flip(other, 0, 1)
        probe_far = flip(near_sum[ET_OWN:], rows, 0)
        own = near_sum + from_far
        probe = jnp.concatenate([own[ET_OWN:], far_sum[ET_OWN:] + probe_far])
        enrol = own[:ET_OWN]
        probe_parts = [probe] + [flip(probe, k, 0) for k in range(1, rows)]
        enrol_parts = []
        for k in range(cols):
            part = flip(enrol, 0, 2 * k) if k else enrol
            enrol_parts += [part, flip(part, 0, 1)]
        return score(n_enrol, n_probe, scale, bias, enrol_parts, probe_parts)

    return jax.shard_map(
        shards,
        mesh=mesh,
        in_specs=(
            P(("groups", "enrol", "probe"), None),
            P(),
            P(),
            P(),
            P(),
            P(("groups", "enrol", "probe")),
            P(("groups", "enrol", "probe"), None),
        ),
        out_specs=P(("groups", "enrol"), "probe"),
        check_vma=False,
    )
```

time: 92.9 us -> 68.6 us (0.74)
  blocking collectives: 23.1 us -> 0 us
  Pallas kernels: 0 us -> 16.5 us
  matrix products: 16 us -> 0 us
  waiting for transfers between devices: 20.3 us -> 30.9 us
  local copies, waits for them, and re-layouts: 12.7 us -> 6.36 us
  other arithmetic: 5.57 us -> 0.09 us
    ppermute x0 -> x14, waiting for transfers between devices: none -> 30.9 us  [flip(): return lax.ppermute(value, ('enrol', 'probe'), pairs)]
    all_gather x2 -> x0, blocking collectives: 23.1 us -> none  [the longest x1 15.2 us: shards(): lax.all_gather(probe_own, 'enrol', axis=0, tiled=True)]
    all_to_all x2 -> x0, waiting for transfers between devices: 20.3 us -> none  [the longest x1 20.3 us: shards(): lax.all_to_all(send_rows, ('enrol', 'probe'), split_axis=0, concat_axis=0...]
    pallas_call x0 -> x4, Pallas kernels: none -> 16.5 us  [the longest x1 13.9 us: embed(): pl.pallas_call(functools.partial(embed_kernel, n_enrol, n_probe), out_sha...]
    dot_general x4 -> x0, matrix products: 16 us -> none  [the longest x1 8.8 us: shards(): jnp.dot(images, w_first, precision=HIGH, preferred_element_type=jnp.float32)]
    all_to_all x2 -> x0, starting transfers between devices: 13.4 us -> none  [the longest x1 7.39 us: shards(): lax.all_to_all(send_slots, ('enrol', 'probe'), split_axis=0, concat_axis=...]
    ppermute x0 -> x14, starting transfers between devices: none -> 12.9 us  [flip(): return lax.ppermute(value, ('enrol', 'probe'), pairs)]
    gather x2 -> x0, local copies, waits for them, and re-layouts: 10.8 us -> none  [the longest x1 6.18 us: shards(): template_slot[picked].reshape(owners, capacity)]
  transfers between devices with their start and end apart: 2 -> 14, of which waited for: 1 -> 9; matrix products, arithmetic and copies ran while one was open for 24% -> 0% of each run, Pallas kernels for 0% -> 1%
where the time goes in v1:
time: 68.6 us; the launch traced here: 68.3 us
  waiting for transfers between devices  30.9 us (45%)
  Pallas kernels  16.5 us (24%)
  starting transfers between devices  12.9 us (19%)
  local copies, waits for them, and re-layouts  6.36 us (9%)
  between operations  1.44 us (2%)
    ppermute x14, waiting for transfers between devices, flip(): return lax.ppermute(value, ('enrol', 'probe'), pairs)  30.9 us
    pallas_call x1, Pallas kernels, embed(): pl.pallas_call(functools.partial(embed_kernel, n_enrol, n_probe), out_sha...  13.9 us
    ppermute x14, starting transfers between devices, flip(): return lax.ppermute(value, ('enrol', 'probe'), pairs)  12.9 us
    unnamed x10, local copies, waits for them, and re-layouts  6.34 us
    pallas_call x1, Pallas kernels, score(): pl.pallas_call(functools.partial(score_kernel, n_enrol, n_probe), out_sha...  1.5 us
  transfers between devices with their start and end apart: 14, of which 9 were waited for; matrix products, arithmetic and copies ran while one was open for 0% of the time, Pallas kernels for 1%

profile of v1, /device:TPU:0, one launch (start us, length us, event | category | flops | bytes accessed | tf_op | source)
XLA Modules:
  0.0 68.3 jit_solution(14504576944019687076)
XLA Ops:
  0.0 2.2 %copy-done = f32[512,2048]{1,0:T(8,128)S(1)} copy-done((f32[512,2048]{1,0:T(8,128)S(1)}, f32[512,2048]{1,0:T(8,128)}, u32[]{:S(2)}) %copy-start) | copy-done | bytes 4194328
  2.2 1.6 %copy-done.1 = f32[2048,256]{1,0:T(8,128)S(1)} copy-done((f32[2048,256]{1,0:T(8,128)S(1)}, f32[2048,256]{1,0:T(8,128)}, u32[]{:S(2)}) %copy-start.1) | copy-done | bytes 2097176
  3.8 1.2 %copy-done.2 = f32[512,512]{1,0:T(8,128)S(1)} copy-done((f32[512,512]{1,0:T(8,128)S(1)}, f32[512,512]{1,0:T(8,128)}, u32[]{:S(2)}) %copy-start.2) | copy-done | bytes 1048600
  5.0 0.7 copy-done.3
  5.7 0.7 copy-done.4
  6.3 13.9 %embed.1 = (f32[136,256]{1,0:T(8,128)S(1)}, f32[136,256]{1,0:T(8,128)S(1)}, f32[136,256]{1,0:T(8,128)S(1)}, f32[136,256]{1,0:T(8,128)S(1)}, f32[128,256]{1,0:T(8...) custom-call(s32[1,16]{1,0:T(1,128)S(1)} %copy-done.4, s32[4,128]{1,0:T(4,128)S(1)} %bitcast.1, ...), custom_call_target="tpu_custom_call" | custom-call | tf_op jit(solution)/shard_map/embed/pallas_call | solution.py:119
  20.2 3.0 %collective-permute-start.3 = (f32[136,256]{1,0:T(8,128)S(1)}, f32[136,256]{1,0:T(8,128)S(1)}, u32[]{:S(2)}, u32[]{:S(2)}) collective-permute-start(f32[136,256]{1,0:T(8,128)S(1)} %get-tuple-element.22), channel_id=1, source_target_pairs={{0,2},{1,3},{2,0},{3,1},{4,6},{5,7},{6,4},{7,5},{8,10},{9,11},{10,... | collective-permute-start | bytes 417800 | tf_op jit(solution)/shard_map/ppermute | solution.py:222
  23.3 1.6 %collective-permute-start.4 = (f32[136,256]{1,0:T(8,128)S(1)}, f32[136,256]{1,0:T(8,128)S(1)}, u32[]{:S(2)}, u32[]{:S(2)}) collective-permute-start(f32[136,256]{1,0:T(8,128)S(1)} %get-tuple-element.23), channel_id=1, source_target_pairs={{0,4},{1,5},{2,6},{3,7},{4,0},{5,1},{6,2},{7,3},{8,12},{9,13},{10,... | collective-permute-start | bytes 417800 | tf_op jit(solution)/shard_map/ppermute | solution.py:222
  24.9 0.0 collective-permute-start.5
  24.9 2.1 %collective-permute-done.3.refs_5_.refs_1_ = f32[136,256]{1,0:T(8,128)S(1)} collective-permute-done((f32[136,256]{1,0:T(8,128)S(1)}, f32[136,256]{1,0:T(8,128)S(1)}, u32[]{:S(2)}, u32[]{:S(2)}) %collective-permute-start.3) | collective-permute-done | bytes 139296 | tf_op jit(solution)/shard_map/ppermute | solution.py:222
  26.9 2.9 %collective-permute-done.4.refs_6_.refs_2_ = f32[136,256]{1,0:T(8,128)S(1)} collective-permute-done((f32[136,256]{1,0:T(8,128)S(1)}, f32[136,256]{1,0:T(8,128)S(1)}, u32[]{:S(2)}, u32[]{:S(2)}) %collective-permute-start.4) | collective-permute-done | bytes 139296 | tf_op jit(solution)/shard_map/ppermute | solution.py:222
  29.8 1.4 %collective-permute-done.5.refs_7_.refs_3_ = f32[136,256]{1,0:T(8,128)S(1)} collective-permute-done((f32[136,256]{1,0:T(8,128)S(1)}, f32[136,256]{1,0:T(8,128)S(1)}, u32[]{:S(2)}, u32[]{:S(2)}) %collective-permute-start.5) | collective-permute-done | bytes 139296 | tf_op jit(solution)/shard_map/ppermute | solution.py:222
  31.2 0.6 pool_far.1
  31.8 0.1 collective-permute-start.7
  31.9 1.7 %collective-permute-start = (f32[128,256]{1,0:T(8,128)S(1)}, f32[128,256]{1,0:T(8,128)S(1)}, u32[]{:S(2)}, u32[]{:S(2)}) collective-permute-start(f32[128,256]{1,0:T(8,128)S(1)} %get-tuple-element.18), channel_id=1, source_target_pairs={{0,2},{1,3},{2,0},{3,1},{4,6},{5,7},{6,4},{7,5},{8,10},{9,11},{10,... | collective-permute-start | bytes 393224 | tf_op jit(solution)/shard_map/ppermute | solution.py:222
  33.6 1.6 %collective-permute-start.1 = (f32[128,256]{1,0:T(8,128)S(1)}, f32[128,256]{1,0:T(8,128)S(1)}, u32[]{:S(2)}, u32[]{:S(2)}) collective-permute-start(f32[128,256]{1,0:T(8,128)S(1)} %get-tuple-element.19), channel_id=1, source_target_pairs={{0,4},{1,5},{2,6},{3,7},{4,0},{5,1},{6,2},{7,3},{8,12},{9,13},{10,... | collective-permute-start | bytes 393224 | tf_op jit(solution)/shard_map/ppermute | solution.py:222
  35.2 0.3 collective-permute-start.2
  35.4 2.3 %collective-permute-done.refs_1_ = f32[128,256]{1,0:T(8,128)S(1)} collective-permute-done((f32[128,256]{1,0:T(8,128)S(1)}, f32[128,256]{1,0:T(8,128)S(1)}, u32[]{:S(2)}, u32[]{:S(2)}) %collective-permute-start) | collective-permute-done | bytes 131104 | tf_op jit(solution)/shard_map/ppermute | solution.py:222
  37.8 2.2 %collective-permute-done.1.refs_2_ = f32[128,256]{1,0:T(8,128)S(1)} collective-permute-done((f32[128,256]{1,0:T(8,128)S(1)}, f32[128,256]{1,0:T(8,128)S(1)}, u32[]{:S(2)}, u32[]{:S(2)}) %collective-permute-start.1) | collective-permute-done | bytes 131104 | tf_op jit(solution)/shard_map/ppermute | solution.py:222
  40.0 1.8 %collective-permute-done.2.refs_3_ = f32[128,256]{1,0:T(8,128)S(1)} collective-permute-done((f32[128,256]{1,0:T(8,128)S(1)}, f32[128,256]{1,0:T(8,128)S(1)}, u32[]{:S(2)}, u32[]{:S(2)}) %collective-permute-start.2) | collective-permute-done | bytes 131104 | tf_op jit(solution)/shard_map/ppermute | solution.py:222
  41.8 0.6 pool_near.1
  42.3 0.1 collective-permute-start.6
  42.5 2.8 %collective-permute-start.8 = (f32[192,256]{1,0:T(8,128)S(1)}, f32[192,256]{1,0:T(8,128)S(1)}, u32[]{:S(2)}, u32[]{:S(2)}) collective-permute-start(f32[192,256]{1,0:T(8,128)S(1)} %add.13), channel_id=1, source_target_pairs={{0,8},{1,9},{2,10},{3,11},{4,12},{5,13},{6,14},{7,15},{8,0},{9,1},... | collective-permute-start | bytes 589832 | tf_op jit(solution)/shard_map/ppermute | solution.py:222
  45.3 9.8 %collective-permute-done.8 = f32[192,256]{1,0:T(8,128)S(1)} collective-permute-done((f32[192,256]{1,0:T(8,128)S(1)}, f32[192,256]{1,0:T(8,128)S(1)}, u32[]{:S(2)}, u32[]{:S(2)}) %collective-permute-start.8) | collective-permute-done | bytes 196640 | tf_op jit(solution)/shard_map/ppermute | solution.py:222
  55.1 0.1 collective-permute-start.12
  55.2 1.6 %collective-permute-start.10 = (f32[128,256]{1,0:T(8,128)S(1)}, f32[128,256]{1,0:T(8,128)S(1)}, u32[]{:S(2)}, u32[]{:S(2)}) collective-permute-start(f32[128,256]{1,0:T(8,128)S(1)} %slice.16.refs_0_), channel_id=1, source_target_pairs={{0,2},{1,3},{2,0},{3,1},{4,6},{5,7},{6,4},{7,5},{8,10},{9,11},{10,... | collective-permute-start | bytes 393224 | tf_op jit(solution)/shard_map/ppermute | solution.py:222
  56.8 0.0 collective-permute-start.9
  56.8 4.9 %collective-permute-done.12 = f32[64,256]{1,0:T(8,128)S(1)} collective-permute-done((f32[64,256]{1,0:T(8,128)S(1)}, f32[64,256]{1,0:T(8,128)S(1)}, u32[]{:S(2)}, u32[]{:S(2)}) %collective-permute-start.12) | collective-permute-done | bytes 65568 | tf_op jit(solution)/shard_map/ppermute | solution.py:222
  61.8 0.1 collective-permute-start.13
  61.8 0.1 collective-permute-start.11
  63.2 3.6 %collective-permute-done.13.refs_5_ = f32[128,256]{1,0:T(8,128)S(1)} collective-permute-done((f32[128,256]{1,0:T(8,128)S(1)}, f32[128,256]{1,0:T(8,128)S(1)}, u32[]{:S(2)}, u32[]{:S(2)}) %collective-permute-start.13) | collective-permute-done | bytes 131104 | tf_op jit(solution)/shard_map/ppermute | solution.py:222
  66.8 1.5 %score.1 = bf16[512,256]{1,0:T(8,128)(2,1)} custom-call(f32[1]{0:T(128)S(6)} %copy.8.scale, f32[1]{0:T(128)S(6)} %copy.9.bias, f32[128,256]{1,0:T(8,128)S(1)} %slice.16.refs_0_, f32[128,256]{1,0:T(8,128)S(1)} %collective-permute-done.9.refs_1_, f32[128,256]{1,0:T(8,128)S(1)} %collective-permute-done.10.refs_2_, ...), custom_call_target="tpu_custom_call" | custom-call | tf_op jit(solution)/shard_map/score/pallas_call | solution.py:200
  (17 shorter events, 0.1 us)
Async XLA Ops:
  0.0 2.2 %copy-start = (f32[512,2048]{1,0:T(8,128)S(1)}, f32[512,2048]{1,0:T(8,128)}, u32[]{:S(2)}) copy-start(f32[512,2048]{1,0:T(8,128)} %w_first.1) | copy-start | bytes 12582916
  2.2 1.6 %copy-start.1 = (f32[2048,256]{1,0:T(8,128)S(1)}, f32[2048,256]{1,0:T(8,128)}, u32[]{:S(2)}) copy-start(f32[2048,256]{1,0:T(8,128)} %w_second.1) | copy-start | bytes 6291460
  3.8 1.2 %copy-start.2 = (f32[512,512]{1,0:T(8,128)S(1)}, f32[512,512]{1,0:T(8,128)}, u32[]{:S(2)}) copy-start(f32[512,512]{1,0:T(8,128)} %images.1) | copy-start | bytes 3145732
  5.0 0.7 copy-start.3
  5.7 0.7 copy-start.4
  20.2 6.7 %collective-permute-start.3 = (f32[136,256]{1,0:T(8,128)S(1)}, f32[136,256]{1,0:T(8,128)S(1)}, u32[]{:S(2)}, u32[]{:S(2)}) collective-permute-start(f32[136,256]{1,0:T(8,128)S(1)} %get-tuple-element.22), channel_id=1, source_target_pairs={{0,2},{1,3},{2,0},{3,1},{4,6},{5,7},{6,4},{7,5},{8,10},{9,11},{10,... | collective-permute-start | bytes 417800 | tf_op jit(solution)/shard_map/ppermute | solution.py:222
  23.3 6.5 %collective-permute-start.4 = (f32[136,256]{1,0:T(8,128)S(1)}, f32[136,256]{1,0:T(8,128)S(1)}, u32[]{:S(2)}, u32[]{:S(2)}) collective-permute-start(f32[136,256]{1,0:T(8,128)S(1)} %get-tuple-element.23), channel_id=1, source_target_pairs={{0,4},{1,5},{2,6},{3,7},{4,0},{5,1},{6,2},{7,3},{8,12},{9,13},{10,... | collective-permute-start | bytes 417800 | tf_op jit(solution)/shard_map/ppermute | solution.py:222
  24.9 6.3 %collective-permute-start.5 = (f32[136,256]{1,0:T(8,128)S(1)}, f32[136,256]{1,0:T(8,128)S(1)}, u32[]{:S(2)}, u32[]{:S(2)}) collective-permute-start(f32[136,256]{1,0:T(8,128)S(1)} %get-tuple-element.24), channel_id=1, source_target_pairs={{0,6},{1,7},{2,4},{3,5},{4,2},{5,3},{6,0},{7,1},{8,14},{9,15},{10,... | collective-permute-start | bytes 417800 | tf_op jit(solution)/shard_map/ppermute | solution.py:222
  31.8 10.6 %collective-permute-start.7 = (f32[192,256]{1,0:T(8,128)S(1)}, f32[192,256]{1,0:T(8,128)S(1)}, u32[]{:S(2)}, u32[]{:S(2)}) collective-permute-start(f32[192,256]{1,0:T(8,128)S(1)} %get-tuple-element.28), channel_id=1, source_target_pairs={{0,1},{1,0},{2,3},{3,2},{4,5},{5,4},{6,7},{7,6},{8,9},{9,8},{10,11... | collective-permute-start | bytes 589832 | tf_op jit(solution)/shard_map/ppermute | solution.py:222
  31.9 5.9 %collective-permute-start = (f32[128,256]{1,0:T(8,128)S(1)}, f32[128,256]{1,0:T(8,128)S(1)}, u32[]{:S(2)}, u32[]{:S(2)}) collective-permute-start(f32[128,256]{1,0:T(8,128)S(1)} %get-tuple-element.18), channel_id=1, source_target_pairs={{0,2},{1,3},{2,0},{3,1},{4,6},{5,7},{6,4},{7,5},{8,10},{9,11},{10,... | collective-permute-start | bytes 393224 | tf_op jit(solution)/shard_map/ppermute | solution.py:222
  33.6 6.4 %collective-permute-start.1 = (f32[128,256]{1,0:T(8,128)S(1)}, f32[128,256]{1,0:T(8,128)S(1)}, u32[]{:S(2)}, u32[]{:S(2)}) collective-permute-start(f32[128,256]{1,0:T(8,128)S(1)} %get-tuple-element.19), channel_id=1, source_target_pairs={{0,4},{1,5},{2,6},{3,7},{4,0},{5,1},{6,2},{7,3},{8,12},{9,13},{10,... | collective-permute-start | bytes 393224 | tf_op jit(solution)/shard_map/ppermute | solution.py:222
  35.2 6.6 %collective-permute-start.2 = (f32[128,256]{1,0:T(8,128)S(1)}, f32[128,256]{1,0:T(8,128)S(1)}, u32[]{:S(2)}, u32[]{:S(2)}) collective-permute-start(f32[128,256]{1,0:T(8,128)S(1)} %get-tuple-element.20), channel_id=1, source_target_pairs={{0,6},{1,7},{2,4},{3,5},{4,2},{5,3},{6,0},{7,1},{8,14},{9,15},{10,... | collective-permute-start | bytes 393224 | tf_op jit(solution)/shard_map/ppermute | solution.py:222
  42.3 2.9 %collective-permute-start.6 = (f32[192,256]{1,0:T(8,128)S(1)}, f32[192,256]{1,0:T(8,128)S(1)}, u32[]{:S(2)}, u32[]{:S(2)}) collective-permute-start(f32[192,256]{1,0:T(8,128)S(1)} %get-tuple-element.26), channel_id=1, source_target_pairs={{0,1},{1,0},{2,3},{3,2},{4,5},{5,4},{6,7},{7,6},{8,9},{9,8},{10,11... | collective-permute-start | bytes 589832 | tf_op jit(solution)/shard_map/ppermute | solution.py:222
  42.5 12.6 %collective-permute-start.8 = (f32[192,256]{1,0:T(8,128)S(1)}, f32[192,256]{1,0:T(8,128)S(1)}, u32[]{:S(2)}, u32[]{:S(2)}) collective-permute-start(f32[192,256]{1,0:T(8,128)S(1)} %add.13), channel_id=1, source_target_pairs={{0,8},{1,9},{2,10},{3,11},{4,12},{5,13},{6,14},{7,15},{8,0},{9,1},... | collective-permute-start | bytes 589832 | tf_op jit(solution)/shard_map/ppermute | solution.py:222
  55.1 6.6 %collective-permute-start.12 = (f32[64,256]{1,0:T(8,128)S(1)}, f32[64,256]{1,0:T(8,128)S(1)}, u32[]{:S(2)}, u32[]{:S(2)}) collective-permute-start(f32[64,256]{1,0:T(8,128)S(1)} %slice.19), channel_id=1, source_target_pairs={{0,8},{1,9},{2,10},{3,11},{4,12},{5,13},{6,14},{7,15},{8,0},{9,1},... | collective-permute-start | bytes 196616 | tf_op jit(solution)/shard_map/ppermute | solution.py:222
  55.2 6.6 %collective-permute-start.10 = (f32[128,256]{1,0:T(8,128)S(1)}, f32[128,256]{1,0:T(8,128)S(1)}, u32[]{:S(2)}, u32[]{:S(2)}) collective-permute-start(f32[128,256]{1,0:T(8,128)S(1)} %slice.16.refs_0_), channel_id=1, source_target_pairs={{0,2},{1,3},{2,0},{3,1},{4,6},{5,7},{6,4},{7,5},{8,10},{9,11},{10,... | collective-permute-start | bytes 393224 | tf_op jit(solution)/shard_map/ppermute | solution.py:222
  56.8 6.4 %collective-permute-start.9 = (f32[128,256]{1,0:T(8,128)S(1)}, f32[128,256]{1,0:T(8,128)S(1)}, u32[]{:S(2)}, u32[]{:S(2)}) collective-permute-start(f32[128,256]{1,0:T(8,128)S(1)} %slice.16.refs_0_), channel_id=1, source_target_pairs={{0,1},{1,0},{2,3},{3,2},{4,5},{5,4},{6,7},{7,6},{8,9},{9,8},{10,11... | collective-permute-start | bytes 393224 | tf_op jit(solution)/shard_map/ppermute | solution.py:222
  61.8 5.0 %collective-permute-start.13 = (f32[128,256]{1,0:T(8,128)S(1)}, f32[128,256]{1,0:T(8,128)S(1)}, u32[]{:S(2)}, u32[]{:S(2)}) collective-permute-start(f32[128,256]{1,0:T(8,128)S(1)} %pad_maximum_fusion.refs_4_), channel_id=1, source_target_pairs={{0,4},{1,5},{2,6},{3,7},{4,0},{5,1},{6,2},{7,3},{8,12},{9,13},{10,... | collective-permute-start | bytes 393224 | tf_op jit(solution)/shard_map/ppermute | solution.py:222
  61.8 4.9 %collective-permute-start.11 = (f32[128,256]{1,0:T(8,128)S(1)}, f32[128,256]{1,0:T(8,128)S(1)}, u32[]{:S(2)}, u32[]{:S(2)}) collective-permute-start(f32[128,256]{1,0:T(8,128)S(1)} %collective-permute-done.10.refs_2_), channel_id=1, source_target_pairs={{0,1},{1,0},{2,3},{3,2},{4,5},{5,4},{6,7},{7,6},{8,9},{9,8},{10,11... | collective-permute-start | bytes 393224 | tf_op jit(solution)/shard_map/ppermute | solution.py:222

commit v2 on v1

--- a/solution.py
+++ b/solution.py
@@ -1,4 +1,5 @@
 import functools
+import math
 
 import jax
 import jax.numpy as jnp
@@ -6,6 +7,7 @@
 from jax.experimental import pallas as pl
 from jax.experimental.pallas import tpu as pltpu
 from jax.sharding import PartitionSpec as P
+
 
 ET_OWN = 128
 PT_OWN = 64
@@ -14,8 +16,10 @@
 EPS = 1e-06
 LANES = 128
 CHUNK = 256
+PIECE = 32
 F32 = jnp.float32
 BF16 = jnp.bfloat16
+ROOT = math.sqrt(2.0 / math.pi)
 
 
 def split(value):
@@ -37,11 +41,19 @@
     return z // rows, (z % rows) * chips + p // 2, p % 2
 
 
-def embed_kernel(n_enrol, n_probe, count, slots, images, w_first, w_second, *rest):
+def gelu(x):
+    inner = x * (ROOT + (ROOT * 0.044715) * (x * x))
+    half = 0.5 * x
+    return half + half * jnp.tanh(inner)
+
+
+def embed_kernel(n_enrol, n_probe, count_hbm, slots_hbm, images, w_first, w_second, *rest):
     chips = n_enrol * n_probe // 4
     owners = n_enrol * n_probe
     far, near = rest[:chips], rest[chips : 2 * chips]
-    (img, w1, w2, emb, table, ends, sem_img, sem_w1, sem_w2) = rest[2 * chips :]
+    (img, w1, w2, x3, w3, pre, h3, v3, feature, emb, slots, table, count, ends, sem_img, sem_w1, sem_w2, sem_small) = rest[
+        2 * chips :
+    ]
     n_img, d_in = images.shape
     width = w_second.shape[1]
     pieces = w1.shape[0]
@@ -52,10 +64,66 @@
     for j in range(pieces):
         a = pltpu.make_async_copy(w_first.at[:, pl.ds(j * CHUNK, CHUNK)], w1.at[j], sem_w1.at[j])
         b = pltpu.make_async_copy(w_second.at[pl.ds(j * CHUNK, CHUNK)], w2.at[j], sem_w2.at[j])
-        a.start()
-        b.start()
         copies.append((a, b))
-
+    copies[0][0].start()
+    small = [
+        pltpu.make_async_copy(count_hbm, count, sem_small.at[0]),
+        pltpu.make_async_copy(slots_hbm, slots, sem_small.at[1]),
+    ]
+    for copy in small:
+        copy.start()
+    for j in range(1, pieces):
+        copies[j][0].start()
+        copies[j - 1][1].start()
+    copies[pieces - 1][1].start()
+
+    copy_img.wait()
+    for r in range(0, n_img, PIECE):
+        at = pl.ds(r, PIECE)
+        high, low = split(img[at, :])
+        x3[at, 0:d_in] = high
+        x3[at, d_in : 2 * d_in] = low
+        x3[at, 2 * d_in :] = high
+
+    def thrice(source, target, rows):
+        for r in range(0, rows, PIECE):
+            high, low = split(source[pl.ds(r, PIECE), :])
+            target[pl.ds(r, PIECE), :] = high
+            target[pl.ds(rows + r, PIECE), :] = high
+            target[pl.ds(2 * rows + r, PIECE), :] = low
+
+    def load(j):
+        copies[j][0].wait()
+        thrice(w1.at[j], w3.at[j % 2], d_in)
+
+    load(0)
+    pre[0] = dot(x3[...], w3[0])
+    load(1)
+
+    def trip(i, carry):
+        for s in range(2):
+            j = 2 * i + s
+            for r in range(0, n_img, PIECE):
+                at = pl.ds(r, PIECE)
+                high, low = split(gelu(pre[s, at, :]))
+                h3[s, at, 0:CHUNK] = high
+                h3[s, at, CHUNK : 2 * CHUNK] = low
+                h3[s, at, 2 * CHUNK :] = high
+            pre[1 - s] = dot(x3[...], w3[1 - s])
+            thrice(w1.at[jnp.minimum(j + 2, pieces - 1)], w3.at[s], d_in)
+            thrice(w2.at[j], v3.at[s], CHUNK)
+            feature[...] = feature[...] + dot(h3[s], v3[s])
+        return carry
+
+    for j in range(pieces):
+        if j > 1:
+            copies[j][0].wait()
+        copies[j][1].wait()
+    feature[...] = jnp.zeros_like(feature)
+    lax.fori_loop(0, pieces // 2, trip, 0)
+
+    for copy in small:
+        copy.wait()
     ends[0] = 0
     rows = slots.shape[0]
     position = lax.broadcasted_iota(jnp.int32, (rows, LANES), 0) * LANES
@@ -69,21 +137,12 @@
     table[...] = jnp.full(table.shape, NONE, jnp.int32)
     table[0:rows, :] = slots[...] + SLOTS * odd
 
-    copy_img.wait()
-    x_high, x_low = split(img[...])
-    feature = jnp.zeros((n_img, width), F32)
-    for j in range(pieces):
-        copies[j][0].wait()
-        w_high, w_low = split(w1[j])
-        pre = dot(x_high, w_high) + dot(x_low, w_high) + dot(x_high, w_low)
-        h_high, h_low = split(jax.nn.gelu(pre))
-        copies[j][1].wait()
-        v_high, v_low = split(w2[j])
-        feature = feature + (dot(h_high, v_high) + dot(h_low, v_high) + dot(h_high, v_low))
-    feature = unit(feature)
     tiles = width // LANES
+    for r in range(0, n_img, PIECE):
+        rows = unit(feature[pl.ds(r, PIECE), :])
+        for t in range(tiles):
+            emb[t, pl.ds(r, PIECE), :] = rows[:, t * LANES : (t + 1) * LANES]
     for t in range(tiles):
-        emb[t, 0:n_img, :] = feature[:, t * LANES : (t + 1) * LANES]
         emb[t, n_img : n_img + block, :] = jnp.zeros((block, LANES), F32)
 
     half, chip, _ = place(n_enrol, n_probe)
@@ -115,62 +174,83 @@
     pieces = w_second.shape[0] // CHUNK
     block = 4 * n_img // (n_enrol * n_probe)
     vmem = pl.BlockSpec(memory_space=pltpu.VMEM)
-    hbm = pl.BlockSpec(memory_space=pl.ANY)
+    hbm = pl.BlockSpec(memory_space=pltpu.HBM)
     outs = pl.pallas_call(
         functools.partial(embed_kernel, n_enrol, n_probe),
         out_shape=[jax.ShapeDtypeStruct((block + 8, width), F32)] * chips
         + [jax.ShapeDtypeStruct((block, width), F32)] * chips,
-        in_specs=[pl.BlockSpec(memory_space=pltpu.SMEM), vmem, hbm, hbm, hbm],
+        in_specs=[hbm] * 5,
         out_specs=[vmem] * (2 * chips),
         scratch_shapes=[
             pltpu.VMEM((n_img, d_in), F32),
             pltpu.VMEM((pieces, d_in, CHUNK), F32),
             pltpu.VMEM((pieces, CHUNK, width), F32),
+            pltpu.VMEM((n_img, 3 * d_in), BF16),
+            pltpu.VMEM((2, 3 * d_in, CHUNK), BF16),
+            pltpu.VMEM((2, n_img, CHUNK), F32),
+            pltpu.VMEM((2, n_img, 3 * CHUNK), BF16),
+            pltpu.VMEM((2, 3 * CHUNK, width), BF16),
+            pltpu.VMEM((n_img, width), F32),
             pltpu.VMEM((width // LANES, n_img + block, LANES), F32),
+            pltpu.VMEM((n_img // LANES, LANES), jnp.int32),
             pltpu.VMEM((n_img // LANES + 8 - n_img // LANES % 8, LANES), jnp.int32),
+            pltpu.SMEM((1, n_enrol * n_probe), jnp.int32),
             pltpu.SMEM((n_enrol * n_probe + 1,), jnp.int32),
             pltpu.SemaphoreType.DMA,
             pltpu.SemaphoreType.DMA((pieces,)),
             pltpu.SemaphoreType.DMA((pieces,)),
+            pltpu.SemaphoreType.DMA((2,)),
         ],
-        compiler_params=pltpu.CompilerParams(vmem_limit_bytes=24 << 20),
+        compiler_params=pltpu.CompilerParams(vmem_limit_bytes=67043328 - (1280 << 10)),
         name="embed",
     )(count, slots.reshape(n_img // LANES, LANES), images, w_first, w_second)
     return outs[:chips], outs[chips:]
 
 
-def pool_kernel(n_enrol, n_probe, side, *refs):
-    chips = n_enrol * n_probe // 4
-    rows, ids = refs[:chips], refs[chips : 2 * chips]
-    mine, other = refs[2 * chips :]
-    _, _, core = place(n_enrol, n_probe)
-    block = rows[0].shape[0] - (0 if side else 8)
-    first = block - 0
+def picked(core, ids, side, rows):
+    block = rows.shape[0] if side else rows.shape[0] - 8
+    at = ids.shape[0] - 8 + side
+    want = ids[at : at + 1, 0:LANES][:, :block].astype(jnp.int32)
+    moved = want - core * SLOTS
+    want = jnp.where((want >= 0) & (moved < 0), moved + 2 * SLOTS, moved)
     slot = lax.broadcasted_iota(jnp.int32, (2 * SLOTS, block), 0)
-    total = jnp.zeros((2 * SLOTS, mine.shape[1]), F32)
-    for k in range(chips):
-        at = first + side
-        want = ids[k][at : at + 1, 0:LANES][:, :block].astype(jnp.int32)
-        moved = want - core * SLOTS
-        want = jnp.where((want >= 0) & (moved < 0), moved + 2 * SLOTS, moved)
-        pick = (slot == want).astype(F32).astype(BF16)
-        high, low = split(rows[k][0:block, :])
-        total = total + dot(pick, high) + dot(pick, low)
-    mine[...] = total[:SLOTS]
-    other[...] = total[SLOTS:]
-
-
-def pool(n_enrol, n_probe, side, rows, ids):
-    width = rows[0].shape[1]
+    pick = (slot == want).astype(F32).astype(BF16)
+    high, low = split(rows[0:block, :])
+    return dot(pick, high) + dot(pick, low)
+
+
+def pool_own_kernel(far, near, far_mine, far_other, near_mine, near_other):
+    core = lax.axis_index("probe") % 2
+    sums = picked(core, far, 0, far)
+    far_mine[...], far_other[...] = sums[:SLOTS], sums[SLOTS:]
+    sums = picked(core, far, 1, near)
+    near_mine[...], near_other[...] = sums[:SLOTS], sums[SLOTS:]
+
+
+def pool_kernel(side, count, *refs):
+    ids, rows = refs[:count], refs[count : 2 * count] if side else refs[:count]
+    mine_before, other_before, mine, other = refs[-4:]
+    core = lax.axis_index("probe") % 2
+    sums = picked(core, ids[0], side, rows[0])
+    for k in range(1, count):
+        sums = sums + picked(core, ids[k], side, rows[k])
+    mine[...] = sums[:SLOTS] + mine_before[...]
+    other[...] = sums[SLOTS:] + other_before[...]
+
+
+def local(kernel, outs, *args, limit=8 << 20):
     vmem = pl.BlockSpec(memory_space=pltpu.VMEM)
     return pl.pallas_call(
-        functools.partial(pool_kernel, n_enrol, n_probe, side),
-        out_shape=[jax.ShapeDtypeStruct((SLOTS, width), F32)] * 2,
-        in_specs=[vmem] * (2 * len(rows)),
-        out_specs=[vmem] * 2,
-        compiler_params=pltpu.CompilerParams(vmem_limit_bytes=8 << 20),
-        name="pool_near" if side else "pool_far",
-    )(*rows, *ids)
+        kernel,
+        out_shape=[jax.ShapeDtypeStruct(shape, F32) for shape in outs],
+        in_specs=[vmem] * len(args),
+        out_specs=[vmem] * len(outs),
+        compiler_params=pltpu.CompilerParams(vmem_limit_bytes=limit),
+    )(*args)
+
+
+def add_kernel(a, b, out):
+    out[...] = a[...] + b[...]
 
 
 def score_kernel(n_enrol, n_probe, scale, bias, *refs):
@@ -222,20 +302,26 @@
         return lax.ppermute(value, ("enrol", "probe"), pairs)
 
     def across_chips(blocks):
-        return [blocks[0]] + [
-            flip(blocks[k], k // cols, 2 * (k % cols)) for k in range(1, chips)
-        ]
-
-    def shards(images, w_first, w_second, scale, bias, template_slot, media_counts):
+        return [flip(blocks[k], k // cols, 2 * (k % cols)) for k in range(1, chips)]
+
+    def body(images, w_first, w_second, scale, bias, template_slot, media_counts):
         far, near = embed(n_enrol, n_probe, images, w_first, w_second, template_slot, media_counts)
-        far = across_chips(far)
-        near = across_chips(near)
-        mine, other = pool(n_enrol, n_probe, 0, far, far)
-        far_sum = mine + flip(other, 0, 1)
+        sums = (SLOTS, w_second.shape[1])
+        far_in = across_chips(far)
+        near_in = across_chips(near)
+        far_mine, far_other, near_mine, near_other = local(
+            pool_own_kernel, [sums] * 4, far[0], near[0]
+        )
+        kernel = functools.partial(pool_kernel, 0, chips - 1)
+        far_mine, far_other = local(kernel, [sums] * 2, *far_in, far_mine, far_other)
+        far_sum = far_mine + flip(far_other, 0, 1)
         from_far = flip(far_sum, rows, 0)
-        mine, other = pool(n_enrol, n_probe, 1, near, far)
-        near_sum = mine + flip(other, 0, 1)
-        probe_far = flip(near_sum[ET_OWN:], rows, 0)
+        kernel = functools.partial(pool_kernel, 1, chips - 1)
+        near_mine, near_other = local(kernel, [sums] * 2, *far_in, *near_in, near_mine, near_other)
+        near_other = flip(near_other, 0, 1)
+        near_probe = near_mine[ET_OWN:] + near_other[ET_OWN:]
+        probe_far = flip(near_probe, rows, 0)
+        (near_sum,) = local(add_kernel, [sums], near_mine, near_other)
         own = near_sum + from_far
         probe = jnp.concatenate([own[ET_OWN:], far_sum[ET_OWN:] + probe_far])
         enrol = own[:ET_OWN]
@@ -247,7 +333,7 @@
         return score(n_enrol, n_probe, scale, bias, enrol_parts, probe_parts)
 
     return jax.shard_map(
-        shards,
+        body,
         mesh=mesh,
         in_specs=(
             P(("groups", "enrol", "probe"), None),

time: 68.6 us -> 52.4 us (0.76)
  waiting for transfers between devices: 30.9 us -> 18 us
  local copies, waits for them, and re-layouts: 6.36 us -> 1.83 us
  starting transfers between devices: 12.9 us -> 16.9 us
  Pallas kernels: 16.5 us -> 14 us
    ppermute x14, waiting for transfers between devices: 30.9 us -> 18 us  [flip(): return lax.ppermute(value, ('enrol', 'probe'), pairs)]
    unnamed x10 -> x4, local copies, waits for them, and re-layouts: 6.34 us -> 1.81 us
    ppermute x14, starting transfers between devices: 12.9 us -> 16.9 us  [flip(): return lax.ppermute(value, ('enrol', 'probe'), pairs)]
    pallas_call x1, Pallas kernels: 13.9 us -> 11.2 us  [embed(): pl.pallas_call(functools.partial(embed_kernel, n_enrol, n_probe), out_sha...]
  transfers between devices with their start and end apart: 14 -> 14, of which waited for: 9 -> 5; matrix products, arithmetic and copies ran while one was open for 0% -> 0% of each run, Pallas kernels for 1% -> 3%
where the time goes in v2:
time: 52.4 us; the launch traced here: 52.3 us
  waiting for transfers between devices  18 us (34%)
  starting transfers between devices  16.9 us (32%)
  Pallas kernels  14 us (27%)
  local copies, waits for them, and re-layouts  1.83 us (3%)
  between operations  1.44 us (3%)
    ppermute x14, waiting for transfers between devices, flip(): return lax.ppermute(value, ('enrol', 'probe'), pairs)  18 us
    ppermute x14, starting transfers between devices, flip(): return lax.ppermute(value, ('enrol', 'probe'), pairs)  16.9 us
    pallas_call x1, Pallas kernels, embed(): pl.pallas_call(functools.partial(embed_kernel, n_enrol, n_probe), out_sha...  11.2 us
    unnamed x4, local copies, waits for them, and re-layouts  1.81 us
    pallas_call x1, Pallas kernels, score(): pl.pallas_call(functools.partial(score_kernel, n_enrol, n_probe), out_sha...  1.5 us
    pallas_call x4, Pallas kernels, local(): pl.pallas_call(kernel, out_shape=[jax.ShapeDtypeStruct(shape, F32) for sh...  1.32 us
  transfers between devices with their start and end apart: 14, of which 5 were waited for; matrix products, arithmetic and copies ran while one was open for 0% of the time, Pallas kernels for 3%

profile of v2, /device:TPU:0, one launch (start us, length us, event | category | flops | bytes accessed | tf_op | source)
XLA Modules:
  0.0 52.3 jit_solution(5699319489559219794)
XLA Ops:
  0.0 11.2 %embed.1 = (f32[136,256]{1,0:T(8,128)}, f32[136,256]{1,0:T(8,128)}, f32[136,256]{1,0:T(8,128)}, f32[136,256]{1,0:T(8,128)}, f32[128,256]{1,0:T(8,128)}, /*index=...) custom-call(s32[1,16]{1,0:T(1,128)} %count_hbm.1, s32[4,128]{1,0:T(4,128)} %bitcast.1, f32[512,512]{1,0:T(8,128)} %images.1, ...), custom_call_target="tpu_custom_call" | custom-call | tf_op jit(solution)/shard_map/embed/pallas_call | solution.py:178
  11.2 3.0 %collective-permute-start = (f32[136,256]{1,0:T(8,128)}, f32[136,256]{1,0:T(8,128)S(1)}, u32[]{:S(2)}, u32[]{:S(2)}) collective-permute-start(f32[136,256]{1,0:T(8,128)} %get-tuple-element.21), channel_id=1, source_target_pairs={{0,2},{1,3},{2,0},{3,1},{4,6},{5,7},{6,4},{7,5},{8,10},{9,11},{10,... | collective-permute-start | bytes 417800 | tf_op jit(solution)/shard_map/ppermute | solution.py:302
  14.2 1.6 %collective-permute-start.1 = (f32[136,256]{1,0:T(8,128)}, f32[136,256]{1,0:T(8,128)S(1)}, u32[]{:S(2)}, u32[]{:S(2)}) collective-permute-start(f32[136,256]{1,0:T(8,128)} %get-tuple-element.22), channel_id=1, source_target_pairs={{0,4},{1,5},{2,6},{3,7},{4,0},{5,1},{6,2},{7,3},{8,12},{9,13},{10,... | collective-permute-start | bytes 417800 | tf_op jit(solution)/shard_map/ppermute | solution.py:302
  15.8 0.0 collective-permute-start.2
  15.8 1.9 %collective-permute-start.3 = (f32[128,256]{1,0:T(8,128)}, f32[128,256]{1,0:T(8,128)S(1)}, u32[]{:S(2)}, u32[]{:S(2)}) collective-permute-start(f32[128,256]{1,0:T(8,128)} %get-tuple-element.24), channel_id=1, source_target_pairs={{0,2},{1,3},{2,0},{3,1},{4,6},{5,7},{6,4},{7,5},{8,10},{9,11},{10,... | collective-permute-start | bytes 393224 | tf_op jit(solution)/shard_map/ppermute | solution.py:302
  17.7 1.6 %collective-permute-start.4 = (f32[128,256]{1,0:T(8,128)}, f32[128,256]{1,0:T(8,128)S(1)}, u32[]{:S(2)}, u32[]{:S(2)}) collective-permute-start(f32[128,256]{1,0:T(8,128)} %get-tuple-element.25), channel_id=1, source_target_pairs={{0,4},{1,5},{2,6},{3,7},{4,0},{5,1},{6,2},{7,3},{8,12},{9,13},{10,... | collective-permute-start | bytes 393224 | tf_op jit(solution)/shard_map/ppermute | solution.py:302
  19.3 0.0 collective-permute-done.refs_0_
  19.3 2.5 %collective-permute-start.5 = (f32[128,256]{1,0:T(8,128)}, f32[128,256]{1,0:T(8,128)S(1)}, u32[]{:S(2)}, u32[]{:S(2)}) collective-permute-start(f32[128,256]{1,0:T(8,128)} %get-tuple-element.26), channel_id=1, source_target_pairs={{0,6},{1,7},{2,4},{3,5},{4,2},{5,3},{6,0},{7,1},{8,14},{9,15},{10,... | collective-permute-start | bytes 393224 | tf_op jit(solution)/shard_map/ppermute | solution.py:302
  21.7 0.9 %copy-done = f32[136,256]{1,0:T(8,128)S(1)} copy-done((f32[136,256]{1,0:T(8,128)S(1)}, f32[136,256]{1,0:T(8,128)}, u32[]{:S(2)}) %copy-start) | copy-done | bytes 139288
  22.6 0.9 %copy-done.1 = f32[128,256]{1,0:T(8,128)S(1)} copy-done((f32[128,256]{1,0:T(8,128)S(1)}, f32[128,256]{1,0:T(8,128)}, u32[]{:S(2)}) %copy-start.1) | copy-done | bytes 131096
  23.5 0.4 shard_map.73
  23.9 0.0 collective-permute-done.2.refs_2_
  23.9 0.5 shard_map.76
  24.4 0.1 collective-permute-start.7
  24.5 2.2 %collective-permute-done.4.refs_4_ = f32[128,256]{1,0:T(8,128)S(1)} collective-permute-done((f32[128,256]{1,0:T(8,128)}, f32[128,256]{1,0:T(8,128)S(1)}, u32[]{:S(2)}, u32[]{:S(2)}) %collective-permute-start.4) | collective-permute-done | bytes 131104 | tf_op jit(solution)/shard_map/ppermute | solution.py:302
  26.8 1.2 %collective-permute-done.5.refs_5_ = f32[128,256]{1,0:T(8,128)S(1)} collective-permute-done((f32[128,256]{1,0:T(8,128)}, f32[128,256]{1,0:T(8,128)S(1)}, u32[]{:S(2)}, u32[]{:S(2)}) %collective-permute-start.5) | collective-permute-done | bytes 131104 | tf_op jit(solution)/shard_map/ppermute | solution.py:302
  28.0 0.5 shard_map.74
  28.5 0.1 collective-permute-start.6
  28.6 2.8 %collective-permute-start.8 = (f32[192,256]{1,0:T(8,128)S(1)}, f32[192,256]{1,0:T(8,128)S(1)}, u32[]{:S(2)}, u32[]{:S(2)}) collective-permute-start(f32[192,256]{1,0:T(8,128)S(1)} %add.12), channel_id=1, source_target_pairs={{0,8},{1,9},{2,10},{3,11},{4,12},{5,13},{6,14},{7,15},{8,0},{9,1},... | collective-permute-start | bytes 589832 | tf_op jit(solution)/shard_map/ppermute | solution.py:302
  31.4 0.0 collective-permute-done.6.b
  31.4 1.4 %collective-permute-start.12 = (f32[64,256]{1,0:T(8,128)S(1)}, f32[64,256]{1,0:T(8,128)S(1)}, u32[]{:S(2)}, u32[]{:S(2)}) collective-permute-start(f32[64,256]{1,0:T(8,128)S(1)} %slice_add_fusion), channel_id=1, source_target_pairs={{0,8},{1,9},{2,10},{3,11},{4,12},{5,13},{6,14},{7,15},{8,0},{9,1},... | collective-permute-start | bytes 196616 | tf_op jit(solution)/shard_map/ppermute | solution.py:302
  32.8 10.1 %collective-permute-done.8 = f32[192,256]{1,0:T(8,128)S(1)} collective-permute-done((f32[192,256]{1,0:T(8,128)S(1)}, f32[192,256]{1,0:T(8,128)S(1)}, u32[]{:S(2)}, u32[]{:S(2)}) %collective-permute-start.8) | collective-permute-done | bytes 196640 | tf_op jit(solution)/shard_map/ppermute | solution.py:302
  43.0 1.7 %collective-permute-start.10 = (f32[128,256]{1,0:T(8,128)S(1)}, f32[128,256]{1,0:T(8,128)S(1)}, u32[]{:S(2)}, u32[]{:S(2)}) collective-permute-start(f32[128,256]{1,0:T(8,128)S(1)} %slice.20.refs_0_), channel_id=1, source_target_pairs={{0,2},{1,3},{2,0},{3,1},{4,6},{5,7},{6,4},{7,5},{8,10},{9,11},{10,... | collective-permute-start | bytes 393224 | tf_op jit(solution)/shard_map/ppermute | solution.py:302
  44.7 0.0 collective-permute-done.12
  44.7 0.1 collective-permute-start.9
  44.8 0.3 collective-permute-start.13
  45.1 2.9 %collective-permute-done.10.refs_2_ = f32[128,256]{1,0:T(8,128)S(1)} collective-permute-done((f32[128,256]{1,0:T(8,128)S(1)}, f32[128,256]{1,0:T(8,128)S(1)}, u32[]{:S(2)}, u32[]{:S(2)}) %collective-permute-start.10) | collective-permute-done | bytes 131104 | tf_op jit(solution)/shard_map/ppermute | solution.py:302
  48.0 0.0 collective-permute-start.11
  49.3 1.4 %collective-permute-done.13.refs_5_ = f32[128,256]{1,0:T(8,128)S(1)} collective-permute-done((f32[128,256]{1,0:T(8,128)S(1)}, f32[128,256]{1,0:T(8,128)S(1)}, u32[]{:S(2)}, u32[]{:S(2)}) %collective-permute-start.13) | collective-permute-done | bytes 131104 | tf_op jit(solution)/shard_map/ppermute | solution.py:302
  50.8 0.0 collective-permute-done.9.refs_1_
  50.8 0.0 collective-permute-done.11.refs_3_
  50.8 1.5 %score.1 = bf16[512,256]{1,0:T(8,128)(2,1)} custom-call(f32[1]{0:T(128)S(6)} %copy.8.scale, f32[1]{0:T(128)S(6)} %copy.9.bias, f32[128,256]{1,0:T(8,128)S(1)} %slice.20.refs_0_, f32[128,256]{1,0:T(8,128)S(1)} %collective-permute-done.9.refs_1_, f32[128,256]{1,0:T(8,128)S(1)} %collective-permute-done.10.refs_2_, ...), custom_call_target="tpu_custom_call" | custom-call | tf_op jit(solution)/shard_map/score/pallas_call | solution.py:280
  (13 shorter events, 0.1 us)
Async XLA Ops:
  11.2 8.1 %collective-permute-start = (f32[136,256]{1,0:T(8,128)}, f32[136,256]{1,0:T(8,128)S(1)}, u32[]{:S(2)}, u32[]{:S(2)}) collective-permute-start(f32[136,256]{1,0:T(8,128)} %get-tuple-element.21), channel_id=1, source_target_pairs={{0,2},{1,3},{2,0},{3,1},{4,6},{5,7},{6,4},{7,5},{8,10},{9,11},{10,... | collective-permute-start | bytes 417800 | tf_op jit(solution)/shard_map/ppermute | solution.py:302
  14.2 9.7 %collective-permute-start.1 = (f32[136,256]{1,0:T(8,128)}, f32[136,256]{1,0:T(8,128)S(1)}, u32[]{:S(2)}, u32[]{:S(2)}) collective-permute-start(f32[136,256]{1,0:T(8,128)} %get-tuple-element.22), channel_id=1, source_target_pairs={{0,4},{1,5},{2,6},{3,7},{4,0},{5,1},{6,2},{7,3},{8,12},{9,13},{10,... | collective-permute-start | bytes 417800 | tf_op jit(solution)/shard_map/ppermute | solution.py:302
  15.8 8.1 %collective-permute-start.2 = (f32[136,256]{1,0:T(8,128)}, f32[136,256]{1,0:T(8,128)S(1)}, u32[]{:S(2)}, u32[]{:S(2)}) collective-permute-start(f32[136,256]{1,0:T(8,128)} %get-tuple-element.23), channel_id=1, source_target_pairs={{0,6},{1,7},{2,4},{3,5},{4,2},{5,3},{6,0},{7,1},{8,14},{9,15},{10,... | collective-permute-start | bytes 417800 | tf_op jit(solution)/shard_map/ppermute | solution.py:302
  15.8 8.7 %collective-permute-start.3 = (f32[128,256]{1,0:T(8,128)}, f32[128,256]{1,0:T(8,128)S(1)}, u32[]{:S(2)}, u32[]{:S(2)}) collective-permute-start(f32[128,256]{1,0:T(8,128)} %get-tuple-element.24), channel_id=1, source_target_pairs={{0,2},{1,3},{2,0},{3,1},{4,6},{5,7},{6,4},{7,5},{8,10},{9,11},{10,... | collective-permute-start | bytes 393224 | tf_op jit(solution)/shard_map/ppermute | solution.py:302
  17.7 9.1 %collective-permute-start.4 = (f32[128,256]{1,0:T(8,128)}, f32[128,256]{1,0:T(8,128)S(1)}, u32[]{:S(2)}, u32[]{:S(2)}) collective-permute-start(f32[128,256]{1,0:T(8,128)} %get-tuple-element.25), channel_id=1, source_target_pairs={{0,4},{1,5},{2,6},{3,7},{4,0},{5,1},{6,2},{7,3},{8,12},{9,13},{10,... | collective-permute-start | bytes 393224 | tf_op jit(solution)/shard_map/ppermute | solution.py:302
  19.3 8.7 %collective-permute-start.5 = (f32[128,256]{1,0:T(8,128)}, f32[128,256]{1,0:T(8,128)S(1)}, u32[]{:S(2)}, u32[]{:S(2)}) collective-permute-start(f32[128,256]{1,0:T(8,128)} %get-tuple-element.26), channel_id=1, source_target_pairs={{0,6},{1,7},{2,4},{3,5},{4,2},{5,3},{6,0},{7,1},{8,14},{9,15},{10,... | collective-permute-start | bytes 393224 | tf_op jit(solution)/shard_map/ppermute | solution.py:302
  21.7 0.9 %copy-start = (f32[136,256]{1,0:T(8,128)S(1)}, f32[136,256]{1,0:T(8,128)}, u32[]{:S(2)}) copy-start(f32[136,256]{1,0:T(8,128)} %get-tuple-element.27.far) | copy-start | bytes 417796
  22.6 0.9 %copy-start.1 = (f32[128,256]{1,0:T(8,128)S(1)}, f32[128,256]{1,0:T(8,128)}, u32[]{:S(2)}) copy-start(f32[128,256]{1,0:T(8,128)} %get-tuple-element.28.near) | copy-start | bytes 393220
  24.4 4.1 %collective-permute-start.7 = (f32[192,256]{1,0:T(8,128)S(1)}, f32[192,256]{1,0:T(8,128)S(1)}, u32[]{:S(2)}, u32[]{:S(2)}) collective-permute-start(f32[192,256]{1,0:T(8,128)S(1)} %get-tuple-element.36), channel_id=1, source_target_pairs={{0,1},{1,0},{2,3},{3,2},{4,5},{5,4},{6,7},{7,6},{8,9},{9,8},{10,11... | collective-permute-start | bytes 589832 | tf_op jit(solution)/shard_map/ppermute | solution.py:302
  28.5 2.9 %collective-permute-start.6 = (f32[192,256]{1,0:T(8,128)S(1)}, f32[192,256]{1,0:T(8,128)S(1)}, u32[]{:S(2)}, u32[]{:S(2)}) collective-permute-start(f32[192,256]{1,0:T(8,128)S(1)} %get-tuple-element.32), channel_id=1, source_target_pairs={{0,1},{1,0},{2,3},{3,2},{4,5},{5,4},{6,7},{7,6},{8,9},{9,8},{10,11... | collective-permute-start | bytes 589832 | tf_op jit(solution)/shard_map/ppermute | solution.py:302
  28.6 14.4 %collective-permute-start.8 = (f32[192,256]{1,0:T(8,128)S(1)}, f32[192,256]{1,0:T(8,128)S(1)}, u32[]{:S(2)}, u32[]{:S(2)}) collective-permute-start(f32[192,256]{1,0:T(8,128)S(1)} %add.12), channel_id=1, source_target_pairs={{0,8},{1,9},{2,10},{3,11},{4,12},{5,13},{6,14},{7,15},{8,0},{9,1},... | collective-permute-start | bytes 589832 | tf_op jit(solution)/shard_map/ppermute | solution.py:302
  31.4 13.3 %collective-permute-start.12 = (f32[64,256]{1,0:T(8,128)S(1)}, f32[64,256]{1,0:T(8,128)S(1)}, u32[]{:S(2)}, u32[]{:S(2)}) collective-permute-start(f32[64,256]{1,0:T(8,128)S(1)} %slice_add_fusion), channel_id=1, source_target_pairs={{0,8},{1,9},{2,10},{3,11},{4,12},{5,13},{6,14},{7,15},{8,0},{9,1},... | collective-permute-start | bytes 196616 | tf_op jit(solution)/shard_map/ppermute | solution.py:302
  43.0 5.0 %collective-permute-start.10 = (f32[128,256]{1,0:T(8,128)S(1)}, f32[128,256]{1,0:T(8,128)S(1)}, u32[]{:S(2)}, u32[]{:S(2)}) collective-permute-start(f32[128,256]{1,0:T(8,128)S(1)} %slice.20.refs_0_), channel_id=1, source_target_pairs={{0,2},{1,3},{2,0},{3,1},{4,6},{5,7},{6,4},{7,5},{8,10},{9,11},{10,... | collective-permute-start | bytes 393224 | tf_op jit(solution)/shard_map/ppermute | solution.py:302
  44.7 6.1 %collective-permute-start.9 = (f32[128,256]{1,0:T(8,128)S(1)}, f32[128,256]{1,0:T(8,128)S(1)}, u32[]{:S(2)}, u32[]{:S(2)}) collective-permute-start(f32[128,256]{1,0:T(8,128)S(1)} %slice.20.refs_0_), channel_id=1, source_target_pairs={{0,1},{1,0},{2,3},{3,2},{4,5},{5,4},{6,7},{7,6},{8,9},{9,8},{10,11... | collective-permute-start | bytes 393224 | tf_op jit(solution)/shard_map/ppermute | solution.py:302
  44.8 6.0 %collective-permute-start.13 = (f32[128,256]{1,0:T(8,128)S(1)}, f32[128,256]{1,0:T(8,128)S(1)}, u32[]{:S(2)}, u32[]{:S(2)}) collective-permute-start(f32[128,256]{1,0:T(8,128)S(1)} %pad_maximum_fusion.refs_4_), channel_id=1, source_target_pairs={{0,4},{1,5},{2,6},{3,7},{4,0},{5,1},{6,2},{7,3},{8,12},{9,13},{10,... | collective-permute-start | bytes 393224 | tf_op jit(solution)/shard_map/ppermute | solution.py:302
  48.0 2.7 %collective-permute-start.11 = (f32[128,256]{1,0:T(8,128)S(1)}, f32[128,256]{1,0:T(8,128)S(1)}, u32[]{:S(2)}, u32[]{:S(2)}) collective-permute-start(f32[128,256]{1,0:T(8,128)S(1)} %collective-permute-done.10.refs_2_), channel_id=1, source_target_pairs={{0,1},{1,0},{2,3},{3,2},{4,5},{5,4},{6,7},{7,6},{8,9},{9,8},{10,11... | collective-permute-start | bytes 393224 | tf_op jit(solution)/shard_map/ppermute | solution.py:302

commit v3 on v2

--- a/solution.py
+++ b/solution.py
@@ -17,6 +17,7 @@
 LANES = 128
 CHUNK = 256
 PIECE = 32
+PER_TRIP = 4
 F32 = jnp.float32
 BF16 = jnp.bfloat16
 ROOT = math.sqrt(2.0 / math.pi)
@@ -77,6 +78,22 @@
         copies[j - 1][1].start()
     copies[pieces - 1][1].start()
 
+    def thrice(source, target, rows):
+        for r in range(0, rows, PIECE):
+            high, low = split(source[pl.ds(r, PIECE), :])
+            target[pl.ds(r, PIECE), :] = high
+            target[pl.ds(rows + r, PIECE), :] = high
+            target[pl.ds(2 * rows + r, PIECE), :] = low
+
+    def first(s):
+        pre[s] = dot(x3[...], w3[s])
+
+    def load(j, s):
+        thrice(w1.at[j], w3.at[s], d_in)
+
+    def bent(s, r):
+        return split(gelu(pre[s, pl.ds(r, PIECE), :]))
+
     copy_img.wait()
     for r in range(0, n_img, PIECE):
         at = pl.ds(r, PIECE)
@@ -84,33 +101,24 @@
         x3[at, 0:d_in] = high
         x3[at, d_in : 2 * d_in] = low
         x3[at, 2 * d_in :] = high
-
-    def thrice(source, target, rows):
-        for r in range(0, rows, PIECE):
-            high, low = split(source[pl.ds(r, PIECE), :])
-            target[pl.ds(r, PIECE), :] = high
-            target[pl.ds(rows + r, PIECE), :] = high
-            target[pl.ds(2 * rows + r, PIECE), :] = low
-
-    def load(j):
-        copies[j][0].wait()
-        thrice(w1.at[j], w3.at[j % 2], d_in)
-
-    load(0)
-    pre[0] = dot(x3[...], w3[0])
-    load(1)
+    copies[0][0].wait()
+    copies[1][0].wait()
+    load(0, 0)
+    first(0)
+    load(1, 1)
+    feature[...] = jnp.zeros_like(feature)
 
     def trip(i, carry):
-        for s in range(2):
-            j = 2 * i + s
+        for step in range(PER_TRIP):
+            j, s = PER_TRIP * i + step, step % 2
             for r in range(0, n_img, PIECE):
                 at = pl.ds(r, PIECE)
-                high, low = split(gelu(pre[s, at, :]))
+                high, low = bent(s, r)
                 h3[s, at, 0:CHUNK] = high
                 h3[s, at, CHUNK : 2 * CHUNK] = low
                 h3[s, at, 2 * CHUNK :] = high
-            pre[1 - s] = dot(x3[...], w3[1 - s])
-            thrice(w1.at[jnp.minimum(j + 2, pieces - 1)], w3.at[s], d_in)
+            first(1 - s)
+            load(jnp.minimum(j + 2, pieces - 1), s)
             thrice(w2.at[j], v3.at[s], CHUNK)
             feature[...] = feature[...] + dot(h3[s], v3[s])
         return carry
@@ -119,8 +127,7 @@
         if j > 1:
             copies[j][0].wait()
         copies[j][1].wait()
-    feature[...] = jnp.zeros_like(feature)
-    lax.fori_loop(0, pieces // 2, trip, 0)
+    lax.fori_loop(0, pieces // PER_TRIP, trip, 0)
 
     for copy in small:
         copy.wait()
@@ -175,6 +182,7 @@
     block = 4 * n_img // (n_enrol * n_probe)
     vmem = pl.BlockSpec(memory_space=pltpu.VMEM)
     hbm = pl.BlockSpec(memory_space=pltpu.HBM)
+    inputs = count, slots.reshape(n_img // LANES, LANES), images, w_first, w_second
     outs = pl.pallas_call(
         functools.partial(embed_kernel, n_enrol, n_probe),
         out_shape=[jax.ShapeDtypeStruct((block + 8, width), F32)] * chips
@@ -201,9 +209,9 @@
             pltpu.SemaphoreType.DMA((pieces,)),
             pltpu.SemaphoreType.DMA((2,)),
         ],
-        compiler_params=pltpu.CompilerParams(vmem_limit_bytes=67043328 - (1280 << 10)),
+        compiler_params=pltpu.CompilerParams(vmem_limit_bytes=52 << 20),
         name="embed",
-    )(count, slots.reshape(n_img // LANES, LANES), images, w_first, w_second)
+    )(*[pltpu.with_memory_space_constraint(x, pltpu.HBM) for x in inputs])
     return outs[:chips], outs[chips:]
 
 
@@ -219,12 +227,14 @@
     return dot(pick, high) + dot(pick, low)
 
 
-def pool_own_kernel(far, near, far_mine, far_other, near_mine, near_other):
-    core = lax.axis_index("probe") % 2
-    sums = picked(core, far, 0, far)
-    far_mine[...], far_other[...] = sums[:SLOTS], sums[SLOTS:]
-    sums = picked(core, far, 1, near)
-    near_mine[...], near_other[...] = sums[:SLOTS], sums[SLOTS:]
+def pool_own_kernel(side, ids, rows, mine, other):
+    sums = picked(lax.axis_index("probe") % 2, ids, side, rows)
+    mine[...], other[...] = sums[:SLOTS], sums[SLOTS:]
+
+
+def pool_one_kernel(half, ids, rows, out):
+    sums = picked(lax.axis_index("probe") % 2, ids, 1, rows)
+    out[...] = sums[SLOTS:] if half else sums[:SLOTS]
 
 
 def pool_kernel(side, count, *refs):
@@ -256,21 +266,25 @@
 def score_kernel(n_enrol, n_probe, scale, bias, *refs):
     rows, cols = n_enrol // 2, n_probe // 2
     enrol, probe = refs[: 2 * cols], refs[2 * cols : 2 * cols + rows]
-    out, table = refs[2 * cols + rows :]
+    out, e3, p3 = refs[2 * cols + rows :]
+    width = enrol[0].shape[1]
     z, p = lax.axis_index("enrol"), lax.axis_index("probe")
+
+    def put(table, start, size, high_low):
+        at = pl.ds(pl.multiple_of(start * size, size), size)
+        for t, part in enumerate(high_low):
+            table[at, t * width : (t + 1) * width] = part
+
     for k in range(rows):
-        own = (z ^ k) * PT_OWN
-        across = (z ^ k ^ rows) * PT_OWN
-        table[pl.ds(pl.multiple_of(own, PT_OWN), PT_OWN), :] = unit(probe[k][0:PT_OWN, :])
-        table[pl.ds(pl.multiple_of(across, PT_OWN), PT_OWN), :] = unit(probe[k][PT_OWN:, :])
-    p_high, p_low = split(table[...])
-    slope, offset = scale[0], bias[0]
-    last = ((1,), (1,))
+        for side in range(2):
+            part = probe[k][side * PT_OWN : (side + 1) * PT_OWN, :]
+            high, low = split(unit(part))
+            put(p3, z ^ k ^ (side * rows), PT_OWN, (high, high, low))
     for k in range(n_probe):
-        e_high, e_low = split(unit(enrol[k][...]))
-        cosine = dot(e_high, p_high, last) + dot(e_low, p_high, last) + dot(e_high, p_low, last)
-        at = pl.multiple_of((p ^ k) * ET_OWN, ET_OWN)
-        out[pl.ds(at, ET_OWN), :] = jax.nn.sigmoid(slope * cosine + offset).astype(BF16)
+        high, low = split(unit(enrol[k][...]))
+        put(e3, p ^ k, ET_OWN, (high, low, high))
+    cosine = dot(e3[...], p3[...], ((1,), (1,)))
+    out[...] = jax.nn.sigmoid(scale[0] * cosine + bias[0]).astype(BF16)
 
 
 def score(n_enrol, n_probe, scale, bias, enrol, probe):
@@ -282,7 +296,10 @@
         out_shape=jax.ShapeDtypeStruct((n_probe * ET_OWN, n_enrol * PT_OWN), BF16),
         in_specs=[smem, smem] + [vmem] * (len(enrol) + len(probe)),
         out_specs=vmem,
-        scratch_shapes=[pltpu.VMEM((n_enrol * PT_OWN, width), F32)],
+        scratch_shapes=[
+            pltpu.VMEM((n_probe * ET_OWN, 3 * width), BF16),
+            pltpu.VMEM((n_enrol * PT_OWN, 3 * width), BF16),
+        ],
         compiler_params=pltpu.CompilerParams(vmem_limit_bytes=8 << 20),
         name="score",
     )(scale, bias, *enrol, *probe)
@@ -302,16 +319,22 @@
         return lax.ppermute(value, ("enrol", "probe"), pairs)
 
     def across_chips(blocks):
-        return [flip(blocks[k], k // cols, 2 * (k % cols)) for k in range(1, chips)]
+        moved = []
+        for k in range(1, chips):
+            moved.append(flip(blocks[k], k // cols, 2 * (k % cols)))
+        return moved
 
     def body(images, w_first, w_second, scale, bias, template_slot, media_counts):
         far, near = embed(n_enrol, n_probe, images, w_first, w_second, template_slot, media_counts)
         sums = (SLOTS, w_second.shape[1])
         far_in = across_chips(far)
         near_in = across_chips(near)
-        far_mine, far_other, near_mine, near_other = local(
-            pool_own_kernel, [sums] * 4, far[0], near[0]
-        )
+        kernel = functools.partial(pool_own_kernel, 0)
+        far_mine, far_other = local(kernel, [sums] * 2, far[0], far[0])
+        kernel = functools.partial(pool_one_kernel, 0)
+        (near_mine,) = local(kernel, [sums], far[0], near[0])
+        kernel = functools.partial(pool_one_kernel, 1)
+        (near_other,) = local(kernel, [sums], far[0], near[0])
         kernel = functools.partial(pool_kernel, 0, chips - 1)
         far_mine, far_other = local(kernel, [sums] * 2, *far_in, far_mine, far_other)
         far_sum = far_mine + flip(far_other, 0, 1)

time: 52.4 us -> 50.3 us (0.960)
  local copies, waits for them, and re-layouts: 1.83 us -> 0.02 us
  Pallas kernels: 14 us -> 12.5 us
  waiting for transfers between devices: 18 us -> 19.4 us
    unnamed x4 -> x0, local copies, waits for them, and re-layouts: 1.81 us -> none
    pallas_call x1, Pallas kernels: 11.2 us -> 9.47 us  [embed(): pl.pallas_call(functools.partial(embed_kernel, n_enrol, n_probe), out_sha...]
    ppermute x14, waiting for transfers between devices: 18 us -> 19.4 us  [flip(): return lax.ppermute(value, ('enrol', 'probe'), pairs)]
    pallas_call x4 -> x6, Pallas kernels: 1.32 us -> 1.69 us  [local(): pl.pallas_call(kernel, out_shape=[jax.ShapeDtypeStruct(shape, F32) for sh...]
  transfers between devices with their start and end apart: 14 -> 14, of which waited for: 5 -> 6; matrix products, arithmetic and copies ran while one was open for 0% -> 0% of each run, Pallas kernels for 3% -> 3%
where the time goes in v3:
time: 50.3 us; the launch traced here: 50.2 us
  waiting for transfers between devices  19.4 us (39%)
  starting transfers between devices  16.7 us (33%)
  Pallas kernels  12.5 us (25%)
  between operations  1.45 us (3%)
    ppermute x14, waiting for transfers between devices, flip(): return lax.ppermute(value, ('enrol', 'probe'), pairs)  19.4 us
    ppermute x14, starting transfers between devices, flip(): return lax.ppermute(value, ('enrol', 'probe'), pairs)  16.7 us
    pallas_call x1, Pallas kernels, embed(): pl.pallas_call(functools.partial(embed_kernel, n_enrol, n_probe), out_sha...  9.47 us
    pallas_call x6, Pallas kernels, local(): pl.pallas_call(kernel, out_shape=[jax.ShapeDtypeStruct(shape, F32) for sh...  1.69 us
    pallas_call x1, Pallas kernels, score(): pl.pallas_call(functools.partial(score_kernel, n_enrol, n_probe), out_sha...  1.29 us
  transfers between devices with their start and end apart: 14, of which 6 were waited for; matrix products, arithmetic and copies ran while one was open for 0% of the time, Pallas kernels for 3%

profile of v3, /device:TPU:0, one launch (start us, length us, event | category | flops | bytes accessed | tf_op | source)
XLA Modules:
  0.0 50.2 jit_solution(2762588560589240915)
XLA Ops:
  0.0 9.5 %embed.1 = (f32[136,256]{1,0:T(8,128)S(1)}, f32[136,256]{1,0:T(8,128)S(1)}, f32[136,256]{1,0:T(8,128)S(1)}, f32[136,256]{1,0:T(8,128)S(1)}, f32[128,256]{1,0:T(8...) custom-call(s32[1,16]{1,0:T(1,128)} %count_hbm.1, s32[4,128]{1,0:T(4,128)} %bitcast.1, ...), custom_call_target="tpu_custom_call" | custom-call | tf_op jit(solution)/shard_map/embed/pallas_call | solution.py:186
  9.5 3.0 %collective-permute-start = (f32[136,256]{1,0:T(8,128)S(1)}, f32[136,256]{1,0:T(8,128)S(1)}, u32[]{:S(2)}, u32[]{:S(2)}) collective-permute-start(f32[136,256]{1,0:T(8,128)S(1)} %get-tuple-element.19), channel_id=1, source_target_pairs={{0,2},{1,3},{2,0},{3,1},{4,6},{5,7},{6,4},{7,5},{8,10},{9,11},{10,... | collective-permute-start | bytes 417800 | tf_op jit(solution)/shard_map/ppermute | solution.py:319
  12.5 1.6 %collective-permute-start.1 = (f32[136,256]{1,0:T(8,128)S(1)}, f32[136,256]{1,0:T(8,128)S(1)}, u32[]{:S(2)}, u32[]{:S(2)}) collective-permute-start(f32[136,256]{1,0:T(8,128)S(1)} %get-tuple-element.20), channel_id=1, source_target_pairs={{0,4},{1,5},{2,6},{3,7},{4,0},{5,1},{6,2},{7,3},{8,12},{9,13},{10,... | collective-permute-start | bytes 417800 | tf_op jit(solution)/shard_map/ppermute | solution.py:319
  14.1 0.0 collective-permute-start.2
  14.1 1.9 %collective-permute-start.3 = (f32[128,256]{1,0:T(8,128)S(1)}, f32[128,256]{1,0:T(8,128)S(1)}, u32[]{:S(2)}, u32[]{:S(2)}) collective-permute-start(f32[128,256]{1,0:T(8,128)S(1)} %get-tuple-element.22), channel_id=1, source_target_pairs={{0,2},{1,3},{2,0},{3,1},{4,6},{5,7},{6,4},{7,5},{8,10},{9,11},{10,... | collective-permute-start | bytes 393224 | tf_op jit(solution)/shard_map/ppermute | solution.py:319
  16.0 1.6 %collective-permute-start.4 = (f32[128,256]{1,0:T(8,128)S(1)}, f32[128,256]{1,0:T(8,128)S(1)}, u32[]{:S(2)}, u32[]{:S(2)}) collective-permute-start(f32[128,256]{1,0:T(8,128)S(1)} %get-tuple-element.23), channel_id=1, source_target_pairs={{0,4},{1,5},{2,6},{3,7},{4,0},{5,1},{6,2},{7,3},{8,12},{9,13},{10,... | collective-permute-start | bytes 393224 | tf_op jit(solution)/shard_map/ppermute | solution.py:319
  17.6 0.0 collective-permute-done.refs_0_
  17.6 2.2 %collective-permute-start.5 = (f32[128,256]{1,0:T(8,128)S(1)}, f32[128,256]{1,0:T(8,128)S(1)}, u32[]{:S(2)}, u32[]{:S(2)}) collective-permute-start(f32[128,256]{1,0:T(8,128)S(1)} %get-tuple-element.24), channel_id=1, source_target_pairs={{0,6},{1,7},{2,4},{3,5},{4,2},{5,3},{6,0},{7,1},{8,14},{9,15},{10,... | collective-permute-start | bytes 393224 | tf_op jit(solution)/shard_map/ppermute | solution.py:319
  19.8 0.2 shard_map.74.refs_7_
  20.1 0.2 shard_map.73.refs_6_
  20.3 0.2 shard_map.77
  20.6 1.0 %collective-permute-done.2.refs_2_ = f32[136,256]{1,0:T(8,128)S(1)} collective-permute-done((f32[136,256]{1,0:T(8,128)S(1)}, f32[136,256]{1,0:T(8,128)S(1)}, u32[]{:S(2)}, u32[]{:S(2)}) %collective-permute-start.2) | collective-permute-done | bytes 139296 | tf_op jit(solution)/shard_map/ppermute | solution.py:319
  21.6 0.5 shard_map.78
  22.1 0.1 collective-permute-start.7
  22.1 2.7 %collective-permute-done.4.refs_4_ = f32[128,256]{1,0:T(8,128)S(1)} collective-permute-done((f32[128,256]{1,0:T(8,128)S(1)}, f32[128,256]{1,0:T(8,128)S(1)}, u32[]{:S(2)}, u32[]{:S(2)}) %collective-permute-start.4) | collective-permute-done | bytes 131104 | tf_op jit(solution)/shard_map/ppermute | solution.py:319
  24.8 1.3 %collective-permute-done.5.refs_5_ = f32[128,256]{1,0:T(8,128)S(1)} collective-permute-done((f32[128,256]{1,0:T(8,128)S(1)}, f32[128,256]{1,0:T(8,128)S(1)}, u32[]{:S(2)}, u32[]{:S(2)}) %collective-permute-start.5) | collective-permute-done | bytes 131104 | tf_op jit(solution)/shard_map/ppermute | solution.py:319
  26.1 0.5 shard_map.75
  26.6 0.1 collective-permute-start.6
  26.7 0.0 collective-permute-done.7
  26.7 2.8 %collective-permute-start.8 = (f32[192,256]{1,0:T(8,128)S(1)}, f32[192,256]{1,0:T(8,128)S(1)}, u32[]{:S(2)}, u32[]{:S(2)}) collective-permute-start(f32[192,256]{1,0:T(8,128)S(1)} %add.12), channel_id=1, source_target_pairs={{0,8},{1,9},{2,10},{3,11},{4,12},{5,13},{6,14},{7,15},{8,0},{9,1},... | collective-permute-start | bytes 589832 | tf_op jit(solution)/shard_map/ppermute | solution.py:319
  29.5 0.0 collective-permute-done.6.b
  29.5 1.4 %collective-permute-start.12 = (f32[64,256]{1,0:T(8,128)S(1)}, f32[64,256]{1,0:T(8,128)S(1)}, u32[]{:S(2)}, u32[]{:S(2)}) collective-permute-start(f32[64,256]{1,0:T(8,128)S(1)} %slice_add_fusion), channel_id=1, source_target_pairs={{0,8},{1,9},{2,10},{3,11},{4,12},{5,13},{6,14},{7,15},{8,0},{9,1},... | collective-permute-start | bytes 196616 | tf_op jit(solution)/shard_map/ppermute | solution.py:319
  30.9 10.1 %collective-permute-done.8 = f32[192,256]{1,0:T(8,128)S(1)} collective-permute-done((f32[192,256]{1,0:T(8,128)S(1)}, f32[192,256]{1,0:T(8,128)S(1)}, u32[]{:S(2)}, u32[]{:S(2)}) %collective-permute-start.8) | collective-permute-done | bytes 196640 | tf_op jit(solution)/shard_map/ppermute | solution.py:319
  41.1 1.7 %collective-permute-start.10 = (f32[128,256]{1,0:T(8,128)S(1)}, f32[128,256]{1,0:T(8,128)S(1)}, u32[]{:S(2)}, u32[]{:S(2)}) collective-permute-start(f32[128,256]{1,0:T(8,128)S(1)} %slice.20.refs_0_), channel_id=1, source_target_pairs={{0,2},{1,3},{2,0},{3,1},{4,6},{5,7},{6,4},{7,5},{8,10},{9,11},{10,... | collective-permute-start | bytes 393224 | tf_op jit(solution)/shard_map/ppermute | solution.py:319
  42.8 0.0 collective-permute-done.12
  42.8 0.1 collective-permute-start.9
  42.9 0.3 collective-permute-start.13
  43.2 2.9 %collective-permute-done.10.refs_2_ = f32[128,256]{1,0:T(8,128)S(1)} collective-permute-done((f32[128,256]{1,0:T(8,128)S(1)}, f32[128,256]{1,0:T(8,128)S(1)}, u32[]{:S(2)}, u32[]{:S(2)}) %collective-permute-start.10) | collective-permute-done | bytes 131104 | tf_op jit(solution)/shard_map/ppermute | solution.py:319
  47.4 1.4 %collective-permute-done.13.refs_5_ = f32[128,256]{1,0:T(8,128)S(1)} collective-permute-done((f32[128,256]{1,0:T(8,128)S(1)}, f32[128,256]{1,0:T(8,128)S(1)}, u32[]{:S(2)}, u32[]{:S(2)}) %collective-permute-start.13) | collective-permute-done | bytes 131104 | tf_op jit(solution)/shard_map/ppermute | solution.py:319
  48.9 0.0 collective-permute-done.9.refs_1_
  48.9 0.0 collective-permute-done.11.refs_3_
  48.9 1.3 %score.1 = bf16[512,256]{1,0:T(8,128)(2,1)} custom-call(f32[1]{0:T(128)S(6)} %copy.8.scale, f32[1]{0:T(128)S(6)} %copy.9.bias, f32[128,256]{1,0:T(8,128)S(1)} %slice.20.refs_0_, f32[128,256]{1,0:T(8,128)S(1)} %collective-permute-done.9.refs_1_, f32[128,256]{1,0:T(8,128)S(1)} %collective-permute-done.10.refs_2_, ...), custom_call_target="tpu_custom_call" | custom-call | tf_op jit(solution)/shard_map/score/pallas_call | solution.py:294
  (11 shorter events, 0.1 us)
Async XLA Ops:
  9.5 8.1 %collective-permute-start = (f32[136,256]{1,0:T(8,128)S(1)}, f32[136,256]{1,0:T(8,128)S(1)}, u32[]{:S(2)}, u32[]{:S(2)}) collective-permute-start(f32[136,256]{1,0:T(8,128)S(1)} %get-tuple-element.19), channel_id=1, source_target_pairs={{0,2},{1,3},{2,0},{3,1},{4,6},{5,7},{6,4},{7,5},{8,10},{9,11},{10,... | collective-permute-start | bytes 417800 | tf_op jit(solution)/shard_map/ppermute | solution.py:319
  12.5 8.1 %collective-permute-start.1 = (f32[136,256]{1,0:T(8,128)S(1)}, f32[136,256]{1,0:T(8,128)S(1)}, u32[]{:S(2)}, u32[]{:S(2)}) collective-permute-start(f32[136,256]{1,0:T(8,128)S(1)} %get-tuple-element.20), channel_id=1, source_target_pairs={{0,4},{1,5},{2,6},{3,7},{4,0},{5,1},{6,2},{7,3},{8,12},{9,13},{10,... | collective-permute-start | bytes 417800 | tf_op jit(solution)/shard_map/ppermute | solution.py:319
  14.1 7.5 %collective-permute-start.2 = (f32[136,256]{1,0:T(8,128)S(1)}, f32[136,256]{1,0:T(8,128)S(1)}, u32[]{:S(2)}, u32[]{:S(2)}) collective-permute-start(f32[136,256]{1,0:T(8,128)S(1)} %get-tuple-element.21), channel_id=1, source_target_pairs={{0,6},{1,7},{2,4},{3,5},{4,2},{5,3},{6,0},{7,1},{8,14},{9,15},{10,... | collective-permute-start | bytes 417800 | tf_op jit(solution)/shard_map/ppermute | solution.py:319
  14.1 8.0 %collective-permute-start.3 = (f32[128,256]{1,0:T(8,128)S(1)}, f32[128,256]{1,0:T(8,128)S(1)}, u32[]{:S(2)}, u32[]{:S(2)}) collective-permute-start(f32[128,256]{1,0:T(8,128)S(1)} %get-tuple-element.22), channel_id=1, source_target_pairs={{0,2},{1,3},{2,0},{3,1},{4,6},{5,7},{6,4},{7,5},{8,10},{9,11},{10,... | collective-permute-start | bytes 393224 | tf_op jit(solution)/shard_map/ppermute | solution.py:319
  16.0 8.8 %collective-permute-start.4 = (f32[128,256]{1,0:T(8,128)S(1)}, f32[128,256]{1,0:T(8,128)S(1)}, u32[]{:S(2)}, u32[]{:S(2)}) collective-permute-start(f32[128,256]{1,0:T(8,128)S(1)} %get-tuple-element.23), channel_id=1, source_target_pairs={{0,4},{1,5},{2,6},{3,7},{4,0},{5,1},{6,2},{7,3},{8,12},{9,13},{10,... | collective-permute-start | bytes 393224 | tf_op jit(solution)/shard_map/ppermute | solution.py:319
  17.6 8.5 %collective-permute-start.5 = (f32[128,256]{1,0:T(8,128)S(1)}, f32[128,256]{1,0:T(8,128)S(1)}, u32[]{:S(2)}, u32[]{:S(2)}) collective-permute-start(f32[128,256]{1,0:T(8,128)S(1)} %get-tuple-element.24), channel_id=1, source_target_pairs={{0,6},{1,7},{2,4},{3,5},{4,2},{5,3},{6,0},{7,1},{8,14},{9,15},{10,... | collective-permute-start | bytes 393224 | tf_op jit(solution)/shard_map/ppermute | solution.py:319
  22.1 4.6 %collective-permute-start.7 = (f32[192,256]{1,0:T(8,128)S(1)}, f32[192,256]{1,0:T(8,128)S(1)}, u32[]{:S(2)}, u32[]{:S(2)}) collective-permute-start(f32[192,256]{1,0:T(8,128)S(1)} %get-tuple-element.32), channel_id=1, source_target_pairs={{0,1},{1,0},{2,3},{3,2},{4,5},{5,4},{6,7},{7,6},{8,9},{9,8},{10,11... | collective-permute-start | bytes 589832 | tf_op jit(solution)/shard_map/ppermute | solution.py:319
  26.6 2.9 %collective-permute-start.6 = (f32[192,256]{1,0:T(8,128)S(1)}, f32[192,256]{1,0:T(8,128)S(1)}, u32[]{:S(2)}, u32[]{:S(2)}) collective-permute-start(f32[192,256]{1,0:T(8,128)S(1)} %get-tuple-element.28), channel_id=1, source_target_pairs={{0,1},{1,0},{2,3},{3,2},{4,5},{5,4},{6,7},{7,6},{8,9},{9,8},{10,11... | collective-permute-start | bytes 589832 | tf_op jit(solution)/shard_map/ppermute | solution.py:319
  26.7 14.4 %collective-permute-start.8 = (f32[192,256]{1,0:T(8,128)S(1)}, f32[192,256]{1,0:T(8,128)S(1)}, u32[]{:S(2)}, u32[]{:S(2)}) collective-permute-start(f32[192,256]{1,0:T(8,128)S(1)} %add.12), channel_id=1, source_target_pairs={{0,8},{1,9},{2,10},{3,11},{4,12},{5,13},{6,14},{7,15},{8,0},{9,1},... | collective-permute-start | bytes 589832 | tf_op jit(solution)/shard_map/ppermute | solution.py:319
  29.5 13.2 %collective-permute-start.12 = (f32[64,256]{1,0:T(8,128)S(1)}, f32[64,256]{1,0:T(8,128)S(1)}, u32[]{:S(2)}, u32[]{:S(2)}) collective-permute-start(f32[64,256]{1,0:T(8,128)S(1)} %slice_add_fusion), channel_id=1, source_target_pairs={{0,8},{1,9},{2,10},{3,11},{4,12},{5,13},{6,14},{7,15},{8,0},{9,1},... | collective-permute-start | bytes 196616 | tf_op jit(solution)/shard_map/ppermute | solution.py:319
  41.1 5.0 %collective-permute-start.10 = (f32[128,256]{1,0:T(8,128)S(1)}, f32[128,256]{1,0:T(8,128)S(1)}, u32[]{:S(2)}, u32[]{:S(2)}) collective-permute-start(f32[128,256]{1,0:T(8,128)S(1)} %slice.20.refs_0_), channel_id=1, source_target_pairs={{0,2},{1,3},{2,0},{3,1},{4,6},{5,7},{6,4},{7,5},{8,10},{9,11},{10,... | collective-permute-start | bytes 393224 | tf_op jit(solution)/shard_map/ppermute | solution.py:319
  42.8 6.1 %collective-permute-start.9 = (f32[128,256]{1,0:T(8,128)S(1)}, f32[128,256]{1,0:T(8,128)S(1)}, u32[]{:S(2)}, u32[]{:S(2)}) collective-permute-start(f32[128,256]{1,0:T(8,128)S(1)} %slice.20.refs_0_), channel_id=1, source_target_pairs={{0,1},{1,0},{2,3},{3,2},{4,5},{5,4},{6,7},{7,6},{8,9},{9,8},{10,11... | collective-permute-start | bytes 393224 | tf_op jit(solution)/shard_map/ppermute | solution.py:319
  42.9 6.0 %collective-permute-start.13 = (f32[128,256]{1,0:T(8,128)S(1)}, f32[128,256]{1,0:T(8,128)S(1)}, u32[]{:S(2)}, u32[]{:S(2)}) collective-permute-start(f32[128,256]{1,0:T(8,128)S(1)} %pad_maximum_fusion.refs_4_), channel_id=1, source_target_pairs={{0,4},{1,5},{2,6},{3,7},{4,0},{5,1},{6,2},{7,3},{8,12},{9,13},{10,... | collective-permute-start | bytes 393224 | tf_op jit(solution)/shard_map/ppermute | solution.py:319
  46.1 2.7 %collective-permute-start.11 = (f32[128,256]{1,0:T(8,128)S(1)}, f32[128,256]{1,0:T(8,128)S(1)}, u32[]{:S(2)}, u32[]{:S(2)}) collective-permute-start(f32[128,256]{1,0:T(8,128)S(1)} %collective-permute-done.10.refs_2_), channel_id=1, source_target_pairs={{0,1},{1,0},{2,3},{3,2},{4,5},{5,4},{6,7},{7,6},{8,9},{9,8},{10,11... | collective-permute-start | bytes 393224 | tf_op jit(solution)/shard_map/ppermute | solution.py:319
